TPU v7x, 32 devices: a whole 2x2x4 slice. The times are simulated.
32 devices in a mesh: groups: 2 (over x), seq: 8 (over z, y), dec: 2 (over core).
Axes of the slice: x: 2, y: 2, z: 4, core: 2. Of those that a mesh axis runs over, the one named last changes fastest.
Arguments:
- tokens: bfloat16 [2048, 4096], P(('groups', 'seq')), parts along dimension 0, may hold values from -64 to 64
- norm_gain: float32 [4096], replicated, may hold values from 0.25 to 1.75
- w_query: bfloat16 [4096, 2048], P('seq', 'dec'), may hold values from -0.140625 to 0.140625
- w_key: bfloat16 [4096, 512], P('seq', 'dec'), may hold values from -0.140625 to 0.140625
- w_value: bfloat16 [4096, 512], P('seq', 'dec'), may hold values from -0.09375 to 0.09375
- block_order: int32 [32], P('groups'), parts along dimension 0, may hold values from 0 to 15, as said below
- block_docs: int32 [32], P('groups'), parts along dimension 0, may hold values from 0 to 3, never falling along the last dimension, each value on 1 to 8 neighbouring positions
- head_owner: int32 [8], P('groups'), parts along dimension 0, may hold values from 0 to 3, as said below
- prev_kv: bfloat16 [2048, 2, 4, 128], P(('groups', 'seq', 'dec')), parts along dimension 0, may hold values from -6 to 6
Outputs:
- attended: bfloat16 [2048, 2048], P(('groups', 'seq'), 'dec'), parts along dimension 0
- decode_cache: bfloat16 [2048, 2, 4, 128], P(('groups', 'seq'), None, 'dec'), parts along dimension 0
There are 2 independent parts, one for each index of `groups`. A program takes and returns all parts, laid end to end along the dimension named above; an argument that names none is the same for every part. Nothing has to cross between parts.
Inputs may be any that keep to these rules, and one draw needn't show every extreme that they name: `block_order`: cycle slots 2i and 2i + 1 hold the blocks b and 15 - b for some b; every block stands in exactly one slot. `head_owner`: each key-value head stands in exactly one decode slot.
All inputs are finite; a program needn't handle non-finite values.
Results may differ from a plain program's by a relative error of at most 0.0035.
The roundings to bfloat16 on the way count: a program that leaves them out, or rounds other values in their place, can miss the bound.
Values may be sent and summed in bfloat16 or wider, within the bound.
No kernel may reach another device: no remote copies, remote signals or barrier semaphores. Data moves between devices by JAX's collectives and lax.ppermute only.
A program may use at most 64 MiB of HBM per device.

v0:
```python
import functools
import math

import jax
import jax.numpy as jnp
from jax import lax
from jax.experimental import pallas as pl
from jax.experimental.pallas import tpu as pltpu
from jax.sharding import PartitionSpec as P


HD = 128
VMEM = pltpu.CompilerParams(vmem_limit_bytes=16 * 2**20)


def place():
    g, i, c = lax.axis_index("groups"), lax.axis_index("seq"), lax.axis_index("dec")
    return g % 2, i, lax.div(i, 2) % 2, c


def sources(order_own, order_other):
    x, i, b, c = place()
    found = []
    for k in range(8):
        grp = x if k % 4 < 2 else 1 - x
        par = b if k % 4 in (0, 2) else 1 - b
        part = c if k < 4 else 1 - c
        slot = (i - 2 * b + 2 * par) * 2 + part
        nat = order_own[slot] if k % 4 < 2 else order_other[slot]
        found.append((nat, grp == b, par * 2 + part))
    return found


def product(lhs_ref, index, blk, start, width):
    depth = blk.shape[0]
    cols = pl.ds(pl.multiple_of(index * depth, depth), depth)
    return jnp.dot(
        lhs_ref[:, cols], blk[:, start : start + width], preferred_element_type=jnp.float32
    )


def gather_kernel(n_tok, kv_masks, q_masks, order_own, order_other, *refs):
    _, i, _, _ = place()
    toks, refs = refs[:n_tok], refs[n_tok:]
    both, refs = refs[: len(q_masks)], refs[len(q_masks) :]
    kvs, refs = refs[: len(kv_masks)], refs[len(kv_masks) :]
    rope, rows, kv_sum, q_sum, spin = refs
    block = toks[0].shape[0]
    for n, tok in enumerate(toks):
        rows[n * block : (n + 1) * block, :] = tok[...]
    for k, (nat, _, _) in enumerate(sources(order_own, order_other)):
        spin[k] = rope[nat]
    width = both[0].shape[1]
    acc = None
    for blk, mask in zip(both, q_masks):
        part = product(rows, i ^ mask, blk, 0, width)
        acc = part if acc is None else acc + part
    q_sum[...] = acc[:, HD:]
    acc = acc[:, :HD]
    for blk, mask in zip(kvs, kv_masks):
        acc = acc + product(rows, i ^ mask, blk, 0, HD)
    kv_sum[...] = acc


def gather(toks, both, q_masks, kvs, kv_masks, orders, rope):
    smem = pl.BlockSpec(memory_space=pltpu.SMEM)
    vmem = pl.BlockSpec(memory_space=pltpu.VMEM)
    block, width = toks[0].shape
    rows = block * len(toks)
    q_width = both[0].shape[1] - HD
    args = list(toks) + list(both) + list(kvs) + [rope]
    return pl.pallas_call(
        functools.partial(gather_kernel, len(toks), kv_masks, q_masks),
        out_shape=[
            pltpu.VMEM((rows, width), jnp.bfloat16),
            pltpu.VMEM((rows, HD), jnp.float32),
            pltpu.VMEM((rows, q_width), jnp.float32),
            pltpu.VMEM((len(toks),) + rope.shape[1:], jnp.float32),
        ],
        in_specs=[smem] * 2 + [vmem] * len(args),
        out_specs=[vmem] * 4,
        compiler_params=VMEM,
        cost_estimate=pl.CostEstimate(flops=2**30, bytes_accessed=2**20, transcendentals=0),
        name="gather_rows",
    )(*orders, *args)


def project_kernel(masks, mode, order_own, order_other, rows, acc_ref, *refs):
    _, i, b, _ = place()
    blks, refs = refs[: len(masks)], refs[len(masks) :]
    acc = acc_ref[...]
    for blk, mask in zip(blks, masks):
        acc = acc + product(rows, i ^ mask, blk, 0, blk.shape[1])
    if mode == "part":
        refs[0][...] = acc
        return
    spin, keep, give = refs
    block, heads = keep.shape[1], keep.shape[2] // HD
    for k, (_, kept, spot) in enumerate(sources(order_own, order_other)):
        cos, sin = spin[k, 0], spin[k, 1]
        tiles = []
        for h in range(heads):
            v = acc[k * block : (k + 1) * block, h * HD : (h + 1) * HD]
            r = v * cos + pltpu.roll(v, HD // 2, 1) * sin
            if mode == "key_value":
                r = jnp.where(b == 0, r, v)
            tiles.append(r.astype(jnp.bfloat16))
        value = tiles[0] if heads == 1 else jnp.concatenate(tiles, axis=1)

        @pl.when(kept)
        def _():
            keep[spot] = value

        @pl.when(jnp.logical_not(kept))
        def _():
            give[spot] = value


def project(mode, rows, acc, blks, masks, orders, spin=None):
    smem = pl.BlockSpec(memory_space=pltpu.SMEM)
    vmem = pl.BlockSpec(memory_space=pltpu.VMEM)
    width = blks[0].shape[1]
    args = [rows, acc] + list(blks) + ([] if spin is None else [spin])
    if mode == "part":
        out_shape = [pltpu.VMEM(acc.shape, jnp.float32)]
    else:
        blocks, _, block, _ = spin.shape
        out_shape = [jax.ShapeDtypeStruct((blocks // 2, block, width), jnp.bfloat16)] * 2
    return pl.pallas_call(
        functools.partial(project_kernel, masks, mode),
        out_shape=out_shape,
        in_specs=[smem] * 2 + [vmem] * len(args),
        out_specs=[vmem] * len(out_shape),
        compiler_params=VMEM,
        cost_estimate=pl.CostEstimate(flops=2**30, bytes_accessed=2**20, transcendentals=0),
    )(*orders, *args)


def norm_kernel(tok, gain, normed):
    v = tok[...].astype(jnp.float32)
    scale = lax.rsqrt(jnp.mean(v * v, axis=-1, keepdims=True) + 1e-05)
    normed[...] = (v * scale * gain[...]).astype(jnp.bfloat16)


def norm(tokens, gain, block, index):
    width = tokens.shape[1]
    return pl.pallas_call(
        norm_kernel,
        grid=(1,),
        out_shape=jax.ShapeDtypeStruct((block, width), jnp.bfloat16),
        in_specs=[
            pl.BlockSpec((block, width), lambda n: (index(), 0)),
            pl.BlockSpec((1, width), lambda n: (0, 0)),
        ],
        out_specs=pl.BlockSpec((block, width), lambda n: (0, 0)),
        compiler_params=VMEM,
        name="norm",
    )(tokens, gain)


def attend_kernel(kv_masks, scale, *refs):
    x, i, b, _ = place()
    order_own, docs_own, order_other, docs_other, query_ref = refs[:5]
    kvs, outs = refs[5:-1], refs[-1:]
    blocks, block, width = query_ref.shape
    heads = width // HD

    def table(own, other, index):
        return jnp.where(x == b, own[index], other[index])

    base = i - 2 * b
    lane = lax.broadcasted_iota(jnp.int32, (1, 2 * block), 1)
    pos_parts, doc_parts = [], []
    for mask in kv_masks:
        for par in range(2):
            slot = ((base ^ mask) + 2 * par) * 2
            n0, n1 = table(order_own, order_other, slot), table(order_own, order_other, slot + 1)
            d0, d1 = table(docs_own, docs_other, n0), table(docs_own, docs_other, n1)
            pos_parts.append(jnp.where(lane < block, n0 * block, (n1 - 1) * block) + lane)
            doc_parts.append(jnp.where(lane < block, d0, d1))
    kpos, kdoc = jnp.concatenate(pos_parts, axis=1), jnp.concatenate(doc_parts, axis=1)
    keys, values = [], []
    for n in range(len(kv_masks)):
        for k in range(blocks):
            kept, got = kvs[2 * n][k], kvs[2 * n + 1][k]
            keys.append(jnp.where(b == 0, kept, got))
            values.append(jnp.where(b == 0, got, kept))
    key, value = jnp.concatenate(keys, axis=0), jnp.concatenate(values, axis=0)
    for k in range(blocks):
        par, part = k // 2, k % 2
        nat = table(order_own, order_other, (base + 2 * par) * 2 + part)
        doc = table(docs_own, docs_other, nat)
        query = jnp.concatenate([query_ref[k, :, h * HD : (h + 1) * HD] for h in range(heads)], axis=0)
        scores = (
            lax.dot_general(query, key, (((1,), (1,)), ((), ())), preferred_element_type=jnp.float32)
            * scale
        )
        qpos = nat * block + lax.broadcasted_iota(jnp.int32, (block, 1), 0)
        bias = jnp.where((kpos <= qpos) & (kdoc == doc), 0.0, -jnp.inf)
        scores = scores + jnp.concatenate([bias] * heads, axis=0)
        row_max = jnp.max(scores, axis=-1, keepdims=True)
        weights = jnp.exp(scores - row_max)
        total = jnp.sum(weights, axis=-1, keepdims=True)
        mixed = jnp.dot(weights.astype(jnp.bfloat16), value, preferred_element_type=jnp.float32) / total
        rows = jnp.concatenate(
            [mixed[h * block : (h + 1) * block].astype(jnp.bfloat16) for h in range(heads)], axis=1
        )
        outs[0][k * block : (k + 1) * block, :] = rows


def attend(tables, query, kvs, kv_masks):
    blocks, block, width = query.shape
    smem = pl.BlockSpec(memory_space=pltpu.SMEM)
    vmem = pl.BlockSpec(memory_space=pltpu.VMEM)
    return pl.pallas_call(
        functools.partial(attend_kernel, kv_masks, 1.0 / math.sqrt(HD)),
        out_shape=jax.ShapeDtypeStruct((blocks * block, width), jnp.bfloat16),
        in_specs=[smem] * len(tables) + [vmem] * (1 + len(kvs)),
        out_specs=vmem,
        compiler_params=VMEM,
        cost_estimate=pl.CostEstimate(flops=10**9, bytes_accessed=10**6, transcendentals=10**6),
    )(*tables, query, *kvs)


def per_device(
    tokens, norm_gain, w_query, w_key, w_value, block_order, block_docs, head_owner, prev_kv
):
    groups, n_seq = lax.axis_size("groups"), lax.axis_size("seq")
    planes = n_seq // 2
    rows_dev = tokens.shape[0]
    slots = block_order.shape[0] // n_seq
    block = rows_dev // slots
    x, _, b, c = place()

    def swap_seq(v, mask):
        return lax.ppermute(v, "seq", [(j, j ^ mask) for j in range(n_seq)])

    def swap_group(v):
        return lax.ppermute(v, "groups", [(j, j ^ 1) for j in range(groups)])

    def swap_core(v):
        return lax.ppermute(v, "dec", [(0, 1), (1, 0)])

    smem = pl.BlockSpec(memory_space=pltpu.SMEM)
    vmem = pl.BlockSpec(memory_space=pltpu.VMEM)
    gain = norm_gain[None, :]
    half = norm(tokens, gain, block, lambda: place()[3])
    rest = norm(tokens, gain, block, lambda: 1 - place()[3])

    n_blocks = block_order.shape[0]
    frequency = 500000.0 ** (-jnp.arange(HD // 2, dtype=jnp.float32) / (HD // 2))
    angles = jnp.arange(n_blocks * block, dtype=jnp.int32).astype(jnp.float32)[:, None] * frequency[None, :]
    cosines, sines = jnp.cos(angles), jnp.sin(angles)
    cos_table = jnp.concatenate([cosines, cosines], -1).reshape(n_blocks, 1, block, HD)
    sin_table = jnp.concatenate([-sines, sines], -1).reshape(n_blocks, 1, block, HD)
    rope = jnp.concatenate([cos_table, sin_table], axis=1)

    own_tables = jnp.concatenate([block_order, block_docs])
    own_tables, rope = lax.optimization_barrier((own_tables, rope))
    other_tables = swap_group(own_tables)
    order_other = other_tables[: block_order.shape[0]]
    docs_other = other_tables[block_order.shape[0] :]

    q_cols = w_query.shape[1] // 4
    keys = lax.dynamic_slice_in_dim(w_key, x * HD, HD, 1)
    values = lax.dynamic_slice_in_dim(w_value, x * HD, HD, 1)
    kv_cols = [jnp.where(b == 0, keys, values), jnp.where(b == 0, values, keys)]
    q_parts = [
        lax.dynamic_slice_in_dim(w_query, (x * 2 + parity) * q_cols, q_cols, 1)
        for parity in (b, 1 - b)
    ]

    tok_z = swap_seq(half, 2)
    tok_x = swap_group(half)
    near = jnp.concatenate([kv_cols[0], q_parts[0]], axis=1)
    both_y0 = swap_seq(near, 1)
    kv_z = [near] + [swap_seq(kv_cols[d % 2], 2 * d) for d in range(1, planes)]
    q_z = [near] + [swap_seq(q_parts[d % 2], 2 * d) for d in range(1, planes)]
    kv_y = [both_y0] + [swap_seq(kv_z[d], 1) for d in range(1, planes)]
    q_y = [both_y0] + [swap_seq(q_z[d], 1) for d in range(1, planes)]
    tok_xz = swap_group(tok_z)
    toks = [half, tok_z, tok_x, tok_xz, rest] + [swap_core(t) for t in (tok_z, tok_x, tok_xz)]

    orders = (block_order, order_other)

    rows, kv_acc, q_acc, spin = gather(
        toks, (near, both_y0), (0, 1), kv_z[1:], [2 * d for d in range(1, planes)], orders, rope
    )
    kv_keep, kv_give = project(
        "key_value", rows, kv_acc, kv_y[1:], [2 * d + 1 for d in range(1, planes)], orders, spin
    )
    kvx_z = [kv_keep] + [swap_seq(kv_give if d % 2 else kv_keep, 2 * d) for d in range(1, planes)]
    kvx_y = [swap_seq(kvx_z[d], 1) for d in range(planes)]
    pairs = range(0, planes, 2)
    kv_masks = [2 * d for d in pairs] + [2 * d + 1 for d in pairs]
    kv_all = [v for part in (kvx_z, kvx_y) for v in part]

    last = 2 if planes > 2 else 1
    (q_acc,) = project(
        "part", rows, q_acc,
        q_z[1:] + [q_y[d] for d in range(1, planes) if d != last],
        [2 * d for d in range(1, planes)] + [2 * d + 1 for d in range(1, planes) if d != last],
        orders,
    )
    q_keep, q_give = project(
        "query", rows, q_acc, [q_y[last]], [2 * last + 1], orders, spin
    )
    q_got = swap_seq(q_give, 2)

    tables = (block_order, block_docs, order_other, docs_other)
    att_keep = attend(tables, q_keep, kv_all, kv_masks)
    att_got = attend(tables, q_got, kv_all, kv_masks)
    att = [att_keep, att_got]
    attended = jnp.concatenate(
        [jnp.where(b == 0, att[0], att[1]), jnp.where(b == 0, att[1], att[0])], axis=1
    )

    first_rows = attended[:rows_dev]
    second_rows = attended[rows_dev:]
    at_b = jnp.where(b == 0, first_rows, second_rows)
    at_other = jnp.where(b == 0, second_rows, first_rows)
    perm_a, perm_b = [], []
    for gg in range(groups):
        for ii in range(n_seq):
            src = gg * n_seq + ii
            if gg % 2 == (ii // 2) % 2:
                perm_a.append((src, gg * n_seq + (ii ^ 2)))
            else:
                perm_a.append((src, (gg ^ 1) * n_seq + ii))
                perm_b.append((src, (gg ^ 1) * n_seq + (ii ^ 2)))
    home = x == b
    from_a = lax.ppermute(jnp.where(home, at_other, at_b), ("groups", "seq"), perm_a)
    from_b = lax.ppermute(at_other, ("groups", "seq"), perm_b)
    same_x = jnp.where(home, at_b, from_a)
    cross_x = jnp.where(home, from_a, from_b)
    out = jnp.concatenate(
        [jnp.where(x == 0, same_x, cross_x), jnp.where(x == 0, cross_x, same_x)], axis=1
    )

    head_count = prev_kv.shape[2]
    selector = (head_owner[:, None] == jnp.arange(head_count, dtype=jnp.int32)[None, :]).astype(
        jnp.bfloat16
    )
    ordered = jnp.einsum(
        "tcjd,sj->tcsd", prev_kv, selector, preferred_element_type=jnp.float32
    ).astype(jnp.bfloat16)
    per_dec = head_count // 2
    stay = jnp.where(c == 0, ordered[:, :, :per_dec], ordered[:, :, per_dec:])
    leave = jnp.where(c == 0, ordered[:, :, per_dec:], ordered[:, :, :per_dec])
    come = swap_core(leave)
    decode_cache = jnp.concatenate(
        [jnp.where(c == 0, stay, come), jnp.where(c == 0, come, stay)], axis=0
    )
    return (out, decode_cache)


def solution(mesh):
    in_specs = (
        P(("groups", "seq"), None),
        P(),
        P("seq", "dec"),
        P("seq", "dec"),
        P("seq", "dec"),
        P("groups"),
        P("groups"),
        P("groups"),
        P(("groups", "seq", "dec"), None, None, None),
    )
    out_specs = (P(("groups", "seq"), "dec"), P(("groups", "seq"), None, "dec", None))

    return jax.shard_map(
        per_device, mesh=mesh, in_specs=in_specs, out_specs=out_specs, check_vma=False
    )
```

profile of v0, /device:TPU:2, one launch (start us, length us, event | category | flops | bytes accessed | tf_op | source)
XLA Modules:
  0.0 110.2 jit_solution(10786874216939296317)
XLA Ops:
  2.9 1.6 %collective-permute-start.1 = (bf16[64,4096]{1,0:T(8,128)(2,1)S(1)}, bf16[64,4096]{1,0:T(8,128)(2,1)}, u32[]{:S(2)}, u32[]{:S(2)}) collective-permute-start(bf16[64,4096]{1,0:T(8,128)(2,1)S(1)} %norm.2.refs_0_), channel_id=1, source_target_pairs={{0,4},{2,6},{4,0},{6,2},{8,12},{10,14},{12,8},{14,10},{1,5},{3,7},... | collective-permute-start | bytes 1572872 | tf_op jit(solution)/shard_map/ppermute | solution.py:236
  5.1 1.9 %multiply_cosine_fusion = (f32[16,1,64,64]{3,2,1,0:T(8,128)S(1)}, f32[16,1,64,64]{3,2,1,0:T(8,128)S(1)}, f32[16,1,64,64]{3,2,1,0:T(8,128)S(1)}) fusion(f32[64]{0:T(128)S(1)} %multiply_power_fusion, f32[16,64]{1,0:T(8,128)S(1)} %add_convert_fusion), kind=kLoop, calls=%fused_computation.4 | loop fusion | flops 131072 | bytes 790784 | tf_op jit(solution)/shard_map/cos | solution.py:253
  9.0 1.7 %broadcast_select_fusion.4 = (bf16[512,128]{1,0:T(8,128)(2,1)}, bf16[512,128]{1,0:T(8,128)(2,1)}) fusion(pred[]{:T(512)S(6)} %eq.19, bf16[512,256]{1,0:T(8,128)(2,1)} %param.13, s32[]{:T(128)S(6)} %select_n.108, bf16[512,256]{1,0:T(8,128)(2,1)} %param.12), kind=kLoop, calls=%fused_computation.17 | loop fusion | flops 131072 | bytes 524293 | tf_op jit(solution)/shard_map/jit(_where)/select_n | solution.py:267
  11.2 2.6 %collective-permute-start.9 = (bf16[512,128]{1,0:T(8,128)(2,1)}, bf16[512,128]{1,0:T(8,128)(2,1)S(1)}, u32[]{:S(2)}, u32[]{:S(2)}) collective-permute-start(bf16[512,128]{1,0:T(8,128)(2,1)} %get-tuple-element.28), channel_id=1, source_target_pairs={{0,8},{2,10},{4,12},{6,14},{8,0},{10,2},{12,4},{14,6},{1,9},{3,11}... | collective-permute-start | bytes 393224 | tf_op jit(solution)/shard_map/ppermute | solution.py:236
  13.8 7.0 %collective-permute-done.1.refs_1_ = bf16[64,4096]{1,0:T(8,128)(2,1)} collective-permute-done((bf16[64,4096]{1,0:T(8,128)(2,1)S(1)}, bf16[64,4096]{1,0:T(8,128)(2,1)}, u32[]{:S(2)}, u32[]{:S(2)}) %collective-permute-start.1) | collective-permute-done | bytes 524320 | tf_op jit(solution)/shard_map/ppermute | solution.py:236
  20.8 1.8 %constant_dynamic-slice_fusion = (bf16[512,256]{1,0:T(8,128)(2,1)}, bf16[512,256]{1,0:T(8,128)(2,1)S(1)}) fusion(bf16[512,1024]{1,0:T(8,128)(2,1)} %param.11, s32[]{:T(128)S(6)} %select_n.112, s32[]{:T(128)S(6)} %select_n.110), kind=kLoop, calls=%fused_computation.32 | loop fusion | bytes 1048584 | tf_op jit(solution)/shard_map/dynamic_slice | solution.py:269
  23.1 4.6 %collective-permute-start.12 = (bf16[512,256]{1,0:T(8,128)(2,1)S(1)}, bf16[512,256]{1,0:T(8,128)(2,1)S(1)}, u32[]{:S(2)}, u32[]{:S(2)}) collective-permute-start(bf16[512,256]{1,0:T(8,128)(2,1)S(1)} %get-tuple-element.26), channel_id=1, source_target_pairs={{0,8},{2,10},{4,12},{6,14},{8,0},{10,2},{12,4},{14,6},{1,9},{3,11}... | collective-permute-start | bytes 786440 | tf_op jit(solution)/shard_map/ppermute | solution.py:236
  27.7 12.1 %collective-permute-done.10.refs_12_ = bf16[512,128]{1,0:T(8,128)(2,1)S(1)} collective-permute-done((bf16[512,128]{1,0:T(8,128)(2,1)}, bf16[512,128]{1,0:T(8,128)(2,1)S(1)}, u32[]{:S(2)}, u32[]{:S(2)}) %collective-permute-start.10) | collective-permute-done | bytes 131104 | tf_op jit(solution)/shard_map/ppermute | solution.py:236
  40.9 1.7 %pad_maximum_fusion.refs_8_ = bf16[512,384]{1,0:T(8,128)(2,1)} fusion(bf16[512,256]{1,0:T(8,128)(2,1)S(1)} %get-tuple-element.26, bf16[512,128]{1,0:T(8,128)(2,1)} %get-tuple-element.28), kind=kLoop, calls=%fused_computation.5 | loop fusion | flops 786432 | bytes 786432 | tf_op jit(solution)/shard_map/concatenate | solution.py:275
  42.6 1.7 %collective-permute-start.7 = (bf16[512,384]{1,0:T(8,128)(2,1)}, bf16[512,384]{1,0:T(8,128)(2,1)}, u32[]{:S(2)}, u32[]{:S(2)}) collective-permute-start(bf16[512,384]{1,0:T(8,128)(2,1)} %pad_maximum_fusion.refs_8_), channel_id=1, source_target_pairs={{0,2},{2,0},{4,6},{6,4},{8,10},{10,8},{12,14},{14,12},{1,3},{3,1},... | collective-permute-start | bytes 1179656 | tf_op jit(solution)/shard_map/ppermute | solution.py:236
  44.8 6.1 %collective-permute-done.13.refs_2_ = bf16[512,256]{1,0:T(8,128)(2,1)} collective-permute-done((bf16[512,256]{1,0:T(8,128)(2,1)}, bf16[512,256]{1,0:T(8,128)(2,1)}, u32[]{:S(2)}, u32[]{:S(2)}) %collective-permute-start.13) | collective-permute-done | bytes 262176 | tf_op jit(solution)/shard_map/ppermute | solution.py:236
  53.3 3.0 %collective-permute-done.17.refs_0_ = bf16[512,128]{1,0:T(8,128)(2,1)S(1)} collective-permute-done((bf16[512,128]{1,0:T(8,128)(2,1)}, bf16[512,128]{1,0:T(8,128)(2,1)S(1)}, u32[]{:S(2)}, u32[]{:S(2)}) %collective-permute-start.17) | collective-permute-done | bytes 131104 | tf_op jit(solution)/shard_map/ppermute | solution.py:236
  56.3 1.7 %collective-permute-start.18 = (bf16[512,128]{1,0:T(8,128)(2,1)}, bf16[512,128]{1,0:T(8,128)(2,1)S(1)}, u32[]{:S(2)}, u32[]{:S(2)}) collective-permute-start(bf16[512,128]{1,0:T(8,128)(2,1)} %copy-done.5), channel_id=1, source_target_pairs={{0,2},{2,0},{4,6},{6,4},{8,10},{10,8},{12,14},{14,12},{1,3},{3,1},... | collective-permute-start | bytes 393224 | tf_op jit(solution)/shard_map/ppermute | solution.py:236
  58.4 1.7 %collective-permute-start.14 = (bf16[512,256]{1,0:T(8,128)(2,1)S(1)}, bf16[512,256]{1,0:T(8,128)(2,1)S(1)}, u32[]{:S(2)}, u32[]{:S(2)}) collective-permute-start(bf16[512,256]{1,0:T(8,128)(2,1)S(1)} %collective-permute-done.11.refs_0_), channel_id=1, source_target_pairs={{0,2},{2,0},{4,6},{6,4},{8,10},{10,8},{12,14},{14,12},{1,3},{3,1},... | collective-permute-start | bytes 786440 | tf_op jit(solution)/shard_map/ppermute | solution.py:236
  61.2 1.7 %collective-permute-start.16 = (bf16[512,256]{1,0:T(8,128)(2,1)}, bf16[512,256]{1,0:T(8,128)(2,1)S(1)}, u32[]{:S(2)}, u32[]{:S(2)}) collective-permute-start(bf16[512,256]{1,0:T(8,128)(2,1)} %copy-done.3), channel_id=1, source_target_pairs={{0,2},{2,0},{4,6},{6,4},{8,10},{10,8},{12,14},{14,12},{1,3},{3,1},... | collective-permute-start | bytes 786440 | tf_op jit(solution)/shard_map/ppermute | solution.py:236
  66.3 3.5 %gather_rows.1 = (bf16[512,4096]{1,0:T(8,128)(2,1)S(1)}, f32[512,128]{1,0:T(8,128)S(1)}, f32[512,256]{1,0:T(8,128)S(1)}, f32[8,2,64,128]{3,2,1,0:T(8,128)S(1)}) custom-call(s32[16]{0:T(128)S(1)} %copy-done.14, s32[16]{0:T(128)S(1)} %get-tuple-element.39.order_other.refs_2_, bf16[64,4096]{1,0:T(8,128)(2,1)S(1)} %norm.2.refs_0_, ...), custom_call_target="tpu_custom_call" | custom-call | flops 1073741824 | bytes 1048576 | tf_op jit(solution)/shard_map/gather_rows/pallas_call | solution.py:72
  69.8 1.7 %shard_map.106 = (bf16[4,64,128]{2,1,0:T(8,128)(2,1)S(1)}, bf16[4,64,128]{2,1,0:T(8,128)(2,1)S(1)}) custom-call(s32[16]{0:T(128)S(1)} %copy-done.14, s32[16]{0:T(128)S(1)} %get-tuple-element.39.order_other.refs_2_, bf16[512,4096]{1,0:T(8,128)(2,1)S(1)} %get-tuple-element.14.rows, f32[512,128]{1,0:T(8,128)S(1)} %get-tuple-element.18.acc_ref, ...), custom_call_target="tpu_custom_call" | custom-call | flops 1073741824 | bytes 1048576 | tf_op jit(solution)/shard_map/pallas_call | solution.py:129
  71.4 6.1 %collective-permute-start.20 = (bf16[4,64,128]{2,1,0:T(8,128)(2,1)S(1)}, bf16[4,64,128]{2,1,0:T(8,128)(2,1)S(1)}, u32[]{:S(2)}, u32[]{:S(2)}) collective-permute-start(bf16[4,64,128]{2,1,0:T(8,128)(2,1)S(1)} %get-tuple-element.20), channel_id=1, source_target_pairs={{0,4},{2,6},{4,0},{6,2},{8,12},{10,14},{12,8},{14,10},{1,5},{3,7},... | collective-permute-start | bytes 196616 | tf_op jit(solution)/shard_map/ppermute | solution.py:236
  79.6 1.8 %shard_map.104.acc_ref = f32[512,256]{1,0:T(8,128)S(1)} custom-call(s32[16]{0:T(128)S(1)} %copy-done.14, s32[16]{0:T(128)S(1)} %get-tuple-element.39.order_other.refs_2_, bf16[512,4096]{1,0:T(8,128)(2,1)S(1)} %get-tuple-element.14.rows, f32[512,256]{1,0:T(8,128)S(1)} %get-tuple-element.15.acc_ref, bf16[512,256]{1,0:T(8,128)(2,1)S(1)} %collective-permute-done.11.refs_0_, ...), custom_call_target="tpu_custom_call" | custom-call | flops 1073741824 | bytes 1048576 | tf_op jit(solution)/shard_map/pallas_call | solution.py:129
  82.9 6.3 %collective-permute-start.27 = (bf16[4,64,256]{2,1,0:T(8,128)(2,1)S(1)}, bf16[4,64,256]{2,1,0:T(8,128)(2,1)S(1)}, u32[]{:S(2)}, u32[]{:S(2)}) collective-permute-start(bf16[4,64,256]{2,1,0:T(8,128)(2,1)S(1)} %get-tuple-element.21), channel_id=1, source_target_pairs={{0,4},{2,6},{4,0},{6,2},{8,12},{10,14},{12,8},{14,10},{1,5},{3,7},... | collective-permute-start | bytes 393224 | tf_op jit(solution)/shard_map/ppermute | solution.py:236
  95.7 2.1 %shard_map.107 = bf16[256,256]{1,0:T(8,128)(2,1)S(1)} custom-call(s32[16]{0:T(128)S(1)} %copy-done.15, s32[16]{0:T(128)S(1)} %copy-done.17, s32[16]{0:T(128)S(1)} %get-tuple-element.39.order_other.refs_2_, s32[16]{0:T(128)S(1)} %get-tuple-element.38.refs_3_, bf16[4,64,256]{2,1,0:T(8,128)(2,1)S(1)} %get-tuple-element.17.refs_4_, ...), custom_call_target="tpu_custom_call" | custom-call | flops 1000000000 | bytes 1000000 | tf_op jit(solution)/shard_map/pallas_call | solution.py:215
  97.9 2.1 %shard_map.108 = bf16[256,256]{1,0:T(8,128)(2,1)S(1)} custom-call(s32[16]{0:T(128)S(1)} %copy-done.15, s32[16]{0:T(128)S(1)} %copy-done.17, s32[16]{0:T(128)S(1)} %get-tuple-element.39.order_other.refs_2_, s32[16]{0:T(128)S(1)} %get-tuple-element.38.refs_3_, bf16[4,64,256]{2,1,0:T(8,128)(2,1)S(1)} %collective-permute-done.27.refs_4_, ...), custom_call_target="tpu_custom_call" | custom-call | flops 1000000000 | bytes 1000000 | tf_op jit(solution)/shard_map/pallas_call | solution.py:215
  101.7 1.9 %collective-permute-start.29 = (bf16[128,512]{1,0:T(8,128)(2,1)S(1)}, bf16[128,512]{1,0:T(8,128)(2,1)S(1)}, u32[]{:S(2)}, u32[]{:S(2)}) collective-permute-start(bf16[128,512]{1,0:T(8,128)(2,1)S(1)} %get-tuple-element.23), channel_id=1, source_target_pairs={{4,16},{6,18},{12,24},{14,26},{16,4},{18,6},{24,12},{26,14},{5,17}... | collective-permute-start | bytes 393224 | tf_op jit(solution)/shard_map/ppermute | solution.py:333
  105.2 4.3 %collective-permute-done.29 = bf16[128,512]{1,0:T(8,128)(2,1)S(1)} collective-permute-done((bf16[128,512]{1,0:T(8,128)(2,1)S(1)}, bf16[128,512]{1,0:T(8,128)(2,1)S(1)}, u32[]{:S(2)}, u32[]{:S(2)}) %collective-permute-start.29) | collective-permute-done | bytes 131104 | tf_op jit(solution)/shard_map/ppermute | solution.py:333
  (105 shorter events, 28.4 us)
Async XLA Ops:
  2.9 17.8 %collective-permute-start.1 = (bf16[64,4096]{1,0:T(8,128)(2,1)S(1)}, bf16[64,4096]{1,0:T(8,128)(2,1)}, u32[]{:S(2)}, u32[]{:S(2)}) collective-permute-start(bf16[64,4096]{1,0:T(8,128)(2,1)S(1)} %norm.2.refs_0_), channel_id=1, source_target_pairs={{0,4},{2,6},{4,0},{6,2},{8,12},{10,14},{12,8},{14,10},{1,5},{3,7},... | collective-permute-start | bytes 1572872 | tf_op jit(solution)/shard_map/ppermute | solution.py:236
  4.6 35.3 %collective-permute-start.2 = (bf16[64,4096]{1,0:T(8,128)(2,1)S(1)}, bf16[64,4096]{1,0:T(8,128)(2,1)}, u32[]{:S(2)}, u32[]{:S(2)}) collective-permute-start(bf16[64,4096]{1,0:T(8,128)(2,1)S(1)} %norm.2.refs_0_), channel_id=1, source_target_pairs={{0,16},{16,0},{1,17},{17,1},{2,18},{18,2},{3,19},{19,3},{4,20},{20... | collective-permute-start | bytes 1572872 | tf_op jit(solution)/shard_map/ppermute | solution.py:239
  7.5 15.1 %collective-permute-start = (s32[32]{0:T(128)S(1)}, s32[32]{0:T(128)S(1)}, u32[]{:S(2)}, u32[]{:S(2)}) collective-permute-start(s32[32]{0:T(128)S(1)} %pad_add_fusion), channel_id=1, source_target_pairs={{0,16},{16,0},{1,17},{17,1},{2,18},{18,2},{3,19},{19,3},{4,20},{20... | collective-permute-start | bytes 392 | tf_op jit(solution)/shard_map/ppermute | solution.py:239
  10.7 12.4 %collective-permute-start.8 = (bf16[512,128]{1,0:T(8,128)(2,1)}, bf16[512,128]{1,0:T(8,128)(2,1)S(1)}, u32[]{:S(2)}, u32[]{:S(2)}) collective-permute-start(bf16[512,128]{1,0:T(8,128)(2,1)} %get-tuple-element.27), channel_id=1, source_target_pairs={{0,4},{2,6},{4,0},{6,2},{8,12},{10,14},{12,8},{14,10},{1,5},{3,7},... | collective-permute-start | bytes 393224 | tf_op jit(solution)/shard_map/ppermute | solution.py:236
  11.2 16.6 %collective-permute-start.9 = (bf16[512,128]{1,0:T(8,128)(2,1)}, bf16[512,128]{1,0:T(8,128)(2,1)S(1)}, u32[]{:S(2)}, u32[]{:S(2)}) collective-permute-start(bf16[512,128]{1,0:T(8,128)(2,1)} %get-tuple-element.28), channel_id=1, source_target_pairs={{0,8},{2,10},{4,12},{6,14},{8,0},{10,2},{12,4},{14,6},{1,9},{3,11}... | collective-permute-start | bytes 393224 | tf_op jit(solution)/shard_map/ppermute | solution.py:236
  20.7 23.7 %collective-permute-start.3 = (bf16[64,4096]{1,0:T(8,128)(2,1)}, bf16[64,4096]{1,0:T(8,128)(2,1)}, u32[]{:S(2)}, u32[]{:S(2)}) collective-permute-start(bf16[64,4096]{1,0:T(8,128)(2,1)} %collective-permute-done.1.refs_1_), channel_id=1, source_target_pairs={{0,16},{16,0},{1,17},{17,1},{2,18},{18,2},{3,19},{19,3},{4,20},{20... | collective-permute-start | bytes 1572872 | tf_op jit(solution)/shard_map/ppermute | solution.py:239
  23.1 17.2 %collective-permute-start.11 = (bf16[512,256]{1,0:T(8,128)(2,1)}, bf16[512,256]{1,0:T(8,128)(2,1)S(1)}, u32[]{:S(2)}, u32[]{:S(2)}) collective-permute-start(bf16[512,256]{1,0:T(8,128)(2,1)} %get-tuple-element.25), channel_id=1, source_target_pairs={{0,4},{2,6},{4,0},{6,2},{8,12},{10,14},{12,8},{14,10},{1,5},{3,7},... | collective-permute-start | bytes 786440 | tf_op jit(solution)/shard_map/ppermute | solution.py:236
  23.1 19.5 %collective-permute-start.12 = (bf16[512,256]{1,0:T(8,128)(2,1)S(1)}, bf16[512,256]{1,0:T(8,128)(2,1)S(1)}, u32[]{:S(2)}, u32[]{:S(2)}) collective-permute-start(bf16[512,256]{1,0:T(8,128)(2,1)S(1)} %get-tuple-element.26), channel_id=1, source_target_pairs={{0,8},{2,10},{4,12},{6,14},{8,0},{10,2},{12,4},{14,6},{1,9},{3,11}... | collective-permute-start | bytes 786440 | tf_op jit(solution)/shard_map/ppermute | solution.py:236
  27.7 12.1 %collective-permute-start.10 = (bf16[512,128]{1,0:T(8,128)(2,1)}, bf16[512,128]{1,0:T(8,128)(2,1)S(1)}, u32[]{:S(2)}, u32[]{:S(2)}) collective-permute-start(bf16[512,128]{1,0:T(8,128)(2,1)} %get-tuple-element.27), channel_id=1, source_target_pairs={{0,12},{2,14},{4,8},{6,10},{8,4},{10,6},{12,0},{14,2},{1,13},{3,15... | collective-permute-start | bytes 393224 | tf_op jit(solution)/shard_map/ppermute | solution.py:236
  39.8 18.5 %collective-permute-start.4 = (bf16[64,4096]{1,0:T(8,128)(2,1)}, bf16[64,4096]{1,0:T(8,128)(2,1)}, u32[]{:S(2)}, u32[]{:S(2)}) collective-permute-start(bf16[64,4096]{1,0:T(8,128)(2,1)} %collective-permute-done.1.refs_1_), channel_id=1, source_target_pairs={{0,1},{1,0},{2,3},{3,2},{4,5},{5,4},{6,7},{7,6},{8,9},{9,8},{10,11... | collective-permute-start | bytes 1572872 | tf_op jit(solution)/shard_map/ppermute | solution.py:242
  39.8 20.3 %collective-permute-start.5 = (bf16[64,4096]{1,0:T(8,128)(2,1)}, bf16[64,4096]{1,0:T(8,128)(2,1)}, u32[]{:S(2)}, u32[]{:S(2)}) collective-permute-start(bf16[64,4096]{1,0:T(8,128)(2,1)} %collective-permute-done.2.refs_2_), channel_id=1, source_target_pairs={{0,1},{1,0},{2,3},{3,2},{4,5},{5,4},{6,7},{7,6},{8,9},{9,8},{10,11... | collective-permute-start | bytes 1572872 | tf_op jit(solution)/shard_map/ppermute | solution.py:242
  42.6 15.4 %collective-permute-start.7 = (bf16[512,384]{1,0:T(8,128)(2,1)}, bf16[512,384]{1,0:T(8,128)(2,1)}, u32[]{:S(2)}, u32[]{:S(2)}) collective-permute-start(bf16[512,384]{1,0:T(8,128)(2,1)} %pad_maximum_fusion.refs_8_), channel_id=1, source_target_pairs={{0,2},{2,0},{4,6},{6,4},{8,10},{10,8},{12,14},{14,12},{1,3},{3,1},... | collective-permute-start | bytes 1179656 | tf_op jit(solution)/shard_map/ppermute | solution.py:236
  44.4 16.8 %collective-permute-start.6 = (bf16[64,4096]{1,0:T(8,128)(2,1)}, bf16[64,4096]{1,0:T(8,128)(2,1)}, u32[]{:S(2)}, u32[]{:S(2)}) collective-permute-start(bf16[64,4096]{1,0:T(8,128)(2,1)} %collective-permute-done.3.refs_3_), channel_id=1, source_target_pairs={{0,1},{1,0},{2,3},{3,2},{4,5},{5,4},{6,7},{7,6},{8,9},{9,8},{10,11... | collective-permute-start | bytes 1572872 | tf_op jit(solution)/shard_map/ppermute | solution.py:242
  56.3 13.4 %collective-permute-start.18 = (bf16[512,128]{1,0:T(8,128)(2,1)}, bf16[512,128]{1,0:T(8,128)(2,1)S(1)}, u32[]{:S(2)}, u32[]{:S(2)}) collective-permute-start(bf16[512,128]{1,0:T(8,128)(2,1)} %copy-done.5), channel_id=1, source_target_pairs={{0,2},{2,0},{4,6},{6,4},{8,10},{10,8},{12,14},{14,12},{1,3},{3,1},... | collective-permute-start | bytes 393224 | tf_op jit(solution)/shard_map/ppermute | solution.py:236
  58.1 11.7 %collective-permute-start.19 = (bf16[512,128]{1,0:T(8,128)(2,1)}, bf16[512,128]{1,0:T(8,128)(2,1)S(1)}, u32[]{:S(2)}, u32[]{:S(2)}) collective-permute-start(bf16[512,128]{1,0:T(8,128)(2,1)} %copy-done.9), channel_id=1, source_target_pairs={{0,2},{2,0},{4,6},{6,4},{8,10},{10,8},{12,14},{14,12},{1,3},{3,1},... | collective-permute-start | bytes 393224 | tf_op jit(solution)/shard_map/ppermute | solution.py:236
  58.4 19.8 %collective-permute-start.14 = (bf16[512,256]{1,0:T(8,128)(2,1)S(1)}, bf16[512,256]{1,0:T(8,128)(2,1)S(1)}, u32[]{:S(2)}, u32[]{:S(2)}) collective-permute-start(bf16[512,256]{1,0:T(8,128)(2,1)S(1)} %collective-permute-done.11.refs_0_), channel_id=1, source_target_pairs={{0,2},{2,0},{4,6},{6,4},{8,10},{10,8},{12,14},{14,12},{1,3},{3,1},... | collective-permute-start | bytes 786440 | tf_op jit(solution)/shard_map/ppermute | solution.py:236
  60.1 19.0 %collective-permute-start.15 = (bf16[512,256]{1,0:T(8,128)(2,1)}, bf16[512,256]{1,0:T(8,128)(2,1)S(1)}, u32[]{:S(2)}, u32[]{:S(2)}) collective-permute-start(bf16[512,256]{1,0:T(8,128)(2,1)} %collective-permute-done.13.refs_2_), channel_id=1, source_target_pairs={{0,2},{2,0},{4,6},{6,4},{8,10},{10,8},{12,14},{14,12},{1,3},{3,1},... | collective-permute-start | bytes 786440 | tf_op jit(solution)/shard_map/ppermute | solution.py:236
  61.2 20.2 %collective-permute-start.16 = (bf16[512,256]{1,0:T(8,128)(2,1)}, bf16[512,256]{1,0:T(8,128)(2,1)S(1)}, u32[]{:S(2)}, u32[]{:S(2)}) collective-permute-start(bf16[512,256]{1,0:T(8,128)(2,1)} %copy-done.3), channel_id=1, source_target_pairs={{0,2},{2,0},{4,6},{6,4},{8,10},{10,8},{12,14},{14,12},{1,3},{3,1},... | collective-permute-start | bytes 786440 | tf_op jit(solution)/shard_map/ppermute | solution.py:236
  71.4 17.8 %collective-permute-start.20 = (bf16[4,64,128]{2,1,0:T(8,128)(2,1)S(1)}, bf16[4,64,128]{2,1,0:T(8,128)(2,1)S(1)}, u32[]{:S(2)}, u32[]{:S(2)}) collective-permute-start(bf16[4,64,128]{2,1,0:T(8,128)(2,1)S(1)} %get-tuple-element.20), channel_id=1, source_target_pairs={{0,4},{2,6},{4,0},{6,2},{8,12},{10,14},{12,8},{14,10},{1,5},{3,7},... | collective-permute-start | bytes 196616 | tf_op jit(solution)/shard_map/ppermute | solution.py:236
  77.5 13.7 %collective-permute-start.22 = (bf16[4,64,128]{2,1,0:T(8,128)(2,1)S(1)}, bf16[4,64,128]{2,1,0:T(8,128)(2,1)S(1)}, u32[]{:S(2)}, u32[]{:S(2)}) collective-permute-start(bf16[4,64,128]{2,1,0:T(8,128)(2,1)S(1)} %get-tuple-element.20), channel_id=1, source_target_pairs={{0,12},{2,14},{4,8},{6,10},{8,4},{10,6},{12,0},{14,2},{1,13},{3,15... | collective-permute-start | bytes 196616 | tf_op jit(solution)/shard_map/ppermute | solution.py:236
  78.2 12.6 %collective-permute-start.21 = (bf16[4,64,128]{2,1,0:T(8,128)(2,1)S(1)}, bf16[4,64,128]{2,1,0:T(8,128)(2,1)S(1)}, u32[]{:S(2)}, u32[]{:S(2)}) collective-permute-start(bf16[4,64,128]{2,1,0:T(8,128)(2,1)S(1)} %get-tuple-element.19.refs_5_), channel_id=1, source_target_pairs={{0,8},{2,10},{4,12},{6,14},{8,0},{10,2},{12,4},{14,6},{1,9},{3,11}... | collective-permute-start | bytes 196616 | tf_op jit(solution)/shard_map/ppermute | solution.py:236
  79.1 13.8 %collective-permute-start.23 = (bf16[4,64,128]{2,1,0:T(8,128)(2,1)S(1)}, bf16[4,64,128]{2,1,0:T(8,128)(2,1)S(1)}, u32[]{:S(2)}, u32[]{:S(2)}) collective-permute-start(bf16[4,64,128]{2,1,0:T(8,128)(2,1)S(1)} %get-tuple-element.19.refs_5_), channel_id=1, source_target_pairs={{0,2},{2,0},{4,6},{6,4},{8,10},{10,8},{12,14},{14,12},{1,3},{3,1},... | collective-permute-start | bytes 196616 | tf_op jit(solution)/shard_map/ppermute | solution.py:236
  82.9 15.0 %collective-permute-start.27 = (bf16[4,64,256]{2,1,0:T(8,128)(2,1)S(1)}, bf16[4,64,256]{2,1,0:T(8,128)(2,1)S(1)}, u32[]{:S(2)}, u32[]{:S(2)}) collective-permute-start(bf16[4,64,256]{2,1,0:T(8,128)(2,1)S(1)} %get-tuple-element.21), channel_id=1, source_target_pairs={{0,4},{2,6},{4,0},{6,2},{8,12},{10,14},{12,8},{14,10},{1,5},{3,7},... | collective-permute-start | bytes 393224 | tf_op jit(solution)/shard_map/ppermute | solution.py:236
  92.9 10.7 %collective-permute-start.30 = (bf16[64,2,2,128]{3,2,1,0:T(2,128)(2,1)S(1)}, bf16[64,2,2,128]{3,2,1,0:T(2,128)(2,1)S(1)}, u32[]{:S(2)}, u32[]{:S(2)}) collective-permute-start(bf16[64,2,2,128]{3,2,1,0:T(2,128)(2,1)S(1)} %broadcast_select_fusion.2), channel_id=1, source_target_pairs={{0,1},{1,0},{2,3},{3,2},{4,5},{5,4},{6,7},{7,6},{8,9},{9,8},{10,11... | collective-permute-start | bytes 196616 | tf_op jit(solution)/shard_map/ppermute | solution.py:242
  (28 other events, 322.5 us)
where the time goes:
time: 111 us; the launch traced here: 110 us
  starting transfers between devices  43 us (39%)
  waiting for transfers between devices  35.7 us (32%)
  Pallas kernels  13.2 us (12%)
  local copies, waits for them, and re-layouts  8.62 us (8%)
  other arithmetic  7.75 us (7%)
    ppermute x22, starting transfers between devices, swap_seq(): return lax.ppermute(v, 'seq', [(j, j ^ mask) for j in range(n_seq)])  36.7 us
    ppermute x22, waiting for transfers between devices, swap_seq(): return lax.ppermute(v, 'seq', [(j, j ^ mask) for j in range(n_seq)])  30.9 us
    unnamed x42, local copies, waits for them, and re-layouts  6.08 us
    pallas_call x3, Pallas kernels, project(): pl.pallas_call(functools.partial(project_kernel, masks, mode), out_shape=...  4.92 us
    pallas_call x2, Pallas kernels, attend(): pl.pallas_call(functools.partial(attend_kernel, kv_masks, 1.0 / math.sqrt...  4.29 us
    ppermute x1, waiting for transfers between devices, per_device(): from_b = lax.ppermute(at_other, ('groups', 'seq'), perm_b)  4.28 us
    pallas_call x1, Pallas kernels, gather(): pl.pallas_call(functools.partial(gather_kernel, len(toks), kv_masks, q_ma...  3.47 us
  transfers between devices with their start and end apart: 31, of which 9 were waited for; matrix products, arithmetic and copies ran while one was open for 9% of the time, Pallas kernels for 12%

commit v1 on v0

--- a/solution.py
+++ b/solution.py
@@ -11,6 +11,8 @@
 
 HD = 128
 VMEM = pltpu.CompilerParams(vmem_limit_bytes=16 * 2**20)
+CUT = None
+COST = pl.CostEstimate(flops=1024, bytes_accessed=1024, transcendentals=0)
 
 
 def place():
@@ -72,27 +74,32 @@
     return pl.pallas_call(
         functools.partial(gather_kernel, len(toks), kv_masks, q_masks),
         out_shape=[
-            pltpu.VMEM((rows, width), jnp.bfloat16),
-            pltpu.VMEM((rows, HD), jnp.float32),
-            pltpu.VMEM((rows, q_width), jnp.float32),
-            pltpu.VMEM((len(toks),) + rope.shape[1:], jnp.float32),
+            jax.ShapeDtypeStruct((rows, width), jnp.bfloat16),
+            jax.ShapeDtypeStruct((rows, HD), jnp.float32),
+            jax.ShapeDtypeStruct((rows, q_width), jnp.float32),
+            jax.ShapeDtypeStruct((len(toks),) + rope.shape[1:], jnp.float32),
         ],
         in_specs=[smem] * 2 + [vmem] * len(args),
         out_specs=[vmem] * 4,
         compiler_params=VMEM,
-        cost_estimate=pl.CostEstimate(flops=2**30, bytes_accessed=2**20, transcendentals=0),
+        cost_estimate=COST,
         name="gather_rows",
     )(*orders, *args)
 
 
-def project_kernel(masks, mode, order_own, order_other, rows, acc_ref, *refs):
+def project_kernel(masks, mode, ahead, order_own, order_other, rows, acc_ref, *refs):
     _, i, b, _ = place()
     blks, refs = refs[: len(masks)], refs[len(masks) :]
     acc = acc_ref[...]
+    depth = blks[0].shape[0]
     for blk, mask in zip(blks, masks):
-        acc = acc + product(rows, i ^ mask, blk, 0, blk.shape[1])
+        index = 0 if rows.shape[1] == depth else i ^ mask
+        acc = acc + product(rows, index, blk, 0, blk.shape[1])
     if mode == "part":
         refs[0][...] = acc
+        if ahead is not None:
+            cols = pl.ds(pl.multiple_of((i ^ ahead) * depth, depth), depth)
+            refs[1][...] = rows[:, cols]
         return
     spin, keep, give = refs
     block, heads = keep.shape[1], keep.shape[2] // HD
@@ -116,24 +123,88 @@
             give[spot] = value
 
 
-def project(mode, rows, acc, blks, masks, orders, spin=None):
+def project(mode, rows, acc, blks, masks, orders, spin=None, ahead=None):
     smem = pl.BlockSpec(memory_space=pltpu.SMEM)
     vmem = pl.BlockSpec(memory_space=pltpu.VMEM)
     width = blks[0].shape[1]
     args = [rows, acc] + list(blks) + ([] if spin is None else [spin])
     if mode == "part":
-        out_shape = [pltpu.VMEM(acc.shape, jnp.float32)]
+        out_shape = [jax.ShapeDtypeStruct(acc.shape, jnp.float32)]
+        if ahead is not None:
+            out_shape.append(jax.ShapeDtypeStruct((rows.shape[0], blks[0].shape[0]), jnp.bfloat16))
     else:
         blocks, _, block, _ = spin.shape
         out_shape = [jax.ShapeDtypeStruct((blocks // 2, block, width), jnp.bfloat16)] * 2
     return pl.pallas_call(
-        functools.partial(project_kernel, masks, mode),
+        functools.partial(project_kernel, masks, mode, ahead),
         out_shape=out_shape,
         in_specs=[smem] * 2 + [vmem] * len(args),
         out_specs=[vmem] * len(out_shape),
         compiler_params=VMEM,
-        cost_estimate=pl.CostEstimate(flops=2**30, bytes_accessed=2**20, transcendentals=0),
+        cost_estimate=COST,
     )(*orders, *args)
+
+
+def cut_kernel(w_query, w_key, w_value, near, kv_same, q_same, kv_other, q_other, sems):
+    x, _, b, _ = place()
+    q_cols = q_other.shape[1]
+    here = pl.ds(pl.multiple_of(x * HD, HD), HD)
+    kv_near = near.at[:, :HD]
+
+    def query(parity):
+        return w_query.at[:, pl.ds(pl.multiple_of((x * 2 + parity) * q_cols, q_cols), q_cols)]
+
+    copies = [
+        pltpu.make_async_copy(query(b), near.at[:, HD:], sems.at[2]),
+        pltpu.make_async_copy(query(b), q_same, sems.at[5]),
+        pltpu.make_async_copy(query(1 - b), q_other, sems.at[3]),
+    ]
+    even = [
+        pltpu.make_async_copy(w_key.at[:, here], kv_near, sems.at[0]),
+        pltpu.make_async_copy(w_key.at[:, here], kv_same, sems.at[4]),
+        pltpu.make_async_copy(w_value.at[:, here], kv_other, sems.at[1]),
+    ]
+    odd = [
+        pltpu.make_async_copy(w_value.at[:, here], kv_near, sems.at[0]),
+        pltpu.make_async_copy(w_value.at[:, here], kv_same, sems.at[4]),
+        pltpu.make_async_copy(w_key.at[:, here], kv_other, sems.at[1]),
+    ]
+
+    @pl.when(b == 0)
+    def _():
+        for copy in even:
+            copy.start()
+
+    @pl.when(b != 0)
+    def _():
+        for copy in odd:
+            copy.start()
+
+    for copy in copies:
+        copy.start()
+    for copy in even + copies:
+        copy.wait()
+
+
+def cut(w_query, w_key, w_value, q_cols):
+    depth = w_query.shape[0]
+    return pl.pallas_call(
+        cut_kernel,
+        out_shape=[
+            jax.ShapeDtypeStruct((depth, HD + q_cols), jnp.bfloat16),
+        ]
+        + [
+            jax.ShapeDtypeStruct((depth, HD), jnp.bfloat16),
+            jax.ShapeDtypeStruct((depth, q_cols), jnp.bfloat16),
+        ]
+        * 2,
+        in_specs=[pl.BlockSpec(memory_space=pl.ANY)] * 3,
+        out_specs=[pl.BlockSpec(memory_space=pltpu.VMEM)] * 5,
+        scratch_shapes=[pltpu.SemaphoreType.DMA((6,))],
+        compiler_params=CUT,
+        cost_estimate=COST,
+        name="cut",
+    )(w_query, w_key, w_value)
 
 
 def norm_kernel(tok, gain, normed):
@@ -142,7 +213,7 @@
     normed[...] = (v * scale * gain[...]).astype(jnp.bfloat16)
 
 
-def norm(tokens, gain, block, index):
+def norm(tokens, gain, block, index, params=VMEM):
     width = tokens.shape[1]
     return pl.pallas_call(
         norm_kernel,
@@ -153,72 +224,80 @@
             pl.BlockSpec((1, width), lambda n: (0, 0)),
         ],
         out_specs=pl.BlockSpec((block, width), lambda n: (0, 0)),
-        compiler_params=VMEM,
+        compiler_params=params,
+        cost_estimate=COST,
         name="norm",
     )(tokens, gain)
 
 
-def attend_kernel(kv_masks, scale, *refs):
+def attend_kernel(kv_masks, scale, first, *refs):
     x, i, b, _ = place()
     order_own, docs_own, order_other, docs_other, query_ref = refs[:5]
-    kvs, outs = refs[5:-1], refs[-1:]
     blocks, block, width = query_ref.shape
     heads = width // HD
+    base = i - 2 * b
 
     def table(own, other, index):
         return jnp.where(x == b, own[index], other[index])
 
-    base = i - 2 * b
-    lane = lax.broadcasted_iota(jnp.int32, (1, 2 * block), 1)
-    pos_parts, doc_parts = [], []
-    for mask in kv_masks:
-        for par in range(2):
-            slot = ((base ^ mask) + 2 * par) * 2
-            n0, n1 = table(order_own, order_other, slot), table(order_own, order_other, slot + 1)
-            d0, d1 = table(docs_own, docs_other, n0), table(docs_own, docs_other, n1)
-            pos_parts.append(jnp.where(lane < block, n0 * block, (n1 - 1) * block) + lane)
-            doc_parts.append(jnp.where(lane < block, d0, d1))
-    kpos, kdoc = jnp.concatenate(pos_parts, axis=1), jnp.concatenate(doc_parts, axis=1)
-    keys, values = [], []
-    for n in range(len(kv_masks)):
-        for k in range(blocks):
-            kept, got = kvs[2 * n][k], kvs[2 * n + 1][k]
-            keys.append(jnp.where(b == 0, kept, got))
-            values.append(jnp.where(b == 0, got, kept))
-    key, value = jnp.concatenate(keys, axis=0), jnp.concatenate(values, axis=0)
+    def natural(mask, k):
+        return table(order_own, order_other, ((base ^ mask) + 2 * (k // 2)) * 2 + k % 2)
+
+    if first:
+        kvs, (out, key_ref, value_ref) = refs[5:-3], refs[-3:]
+        for n, mask in enumerate(kv_masks):
+            for k in range(blocks):
+                kept, got = kvs[2 * n][k], kvs[2 * n + 1][k]
+                nat = natural(mask, k)
+                key_ref[nat] = jnp.where(b == 0, kept, got)
+                value_ref[nat] = jnp.where(b == 0, got, kept)
+    else:
+        key_ref, value_ref, out = refs[5:]
+    total_blocks = key_ref.shape[0]
+    window = total_blocks // 2
+    lane = lax.broadcasted_iota(jnp.int32, (1, window * block), 1)
+    row = lax.broadcasted_iota(jnp.int32, (block, 1), 0)
     for k in range(blocks):
-        par, part = k // 2, k % 2
-        nat = table(order_own, order_other, (base + 2 * par) * 2 + part)
+        nat = natural(0, k)
         doc = table(docs_own, docs_other, nat)
+        start = jnp.maximum(nat - (window - 1), 0)
+        opening = jnp.int32(0)
+        for n in range(total_blocks):
+            opening += (table(docs_own, docs_other, n) < doc).astype(jnp.int32)
+        key = key_ref[pl.ds(start, window)].reshape(window * block, HD)
+        value = value_ref[pl.ds(start, window)].reshape(window * block, HD)
         query = jnp.concatenate([query_ref[k, :, h * HD : (h + 1) * HD] for h in range(heads)], axis=0)
-        scores = (
-            lax.dot_general(query, key, (((1,), (1,)), ((), ())), preferred_element_type=jnp.float32)
-            * scale
+        scores = lax.dot_general(
+            query, key, (((1,), (1,)), ((), ())), preferred_element_type=jnp.float32
         )
-        qpos = nat * block + lax.broadcasted_iota(jnp.int32, (block, 1), 0)
-        bias = jnp.where((kpos <= qpos) & (kdoc == doc), 0.0, -jnp.inf)
+        key_pos = start * block + lane
+        allowed = (key_pos <= nat * block + row) & (key_pos >= opening * block)
+        bias = jnp.where(allowed, 0.0, -jnp.inf)
         scores = scores + jnp.concatenate([bias] * heads, axis=0)
         row_max = jnp.max(scores, axis=-1, keepdims=True)
-        weights = jnp.exp(scores - row_max)
+        weights = jnp.exp2((scores - row_max) * (scale * math.log2(math.e)))
         total = jnp.sum(weights, axis=-1, keepdims=True)
         mixed = jnp.dot(weights.astype(jnp.bfloat16), value, preferred_element_type=jnp.float32) / total
-        rows = jnp.concatenate(
+        out[k * block : (k + 1) * block, :] = jnp.concatenate(
             [mixed[h * block : (h + 1) * block].astype(jnp.bfloat16) for h in range(heads)], axis=1
         )
-        outs[0][k * block : (k + 1) * block, :] = rows
-
-
-def attend(tables, query, kvs, kv_masks):
+
+
+def attend(first, tables, query, kvs, kv_masks):
     blocks, block, width = query.shape
     smem = pl.BlockSpec(memory_space=pltpu.SMEM)
     vmem = pl.BlockSpec(memory_space=pltpu.VMEM)
+    out_shape = [jax.ShapeDtypeStruct((blocks * block, width), jnp.bfloat16)]
+    if first:
+        out_shape += [jax.ShapeDtypeStruct((tables[0].shape[0], block, HD), jnp.bfloat16)] * 2
     return pl.pallas_call(
-        functools.partial(attend_kernel, kv_masks, 1.0 / math.sqrt(HD)),
-        out_shape=jax.ShapeDtypeStruct((blocks * block, width), jnp.bfloat16),
+        functools.partial(attend_kernel, kv_masks, 1.0 / math.sqrt(HD), first),
+        out_shape=out_shape,
         in_specs=[smem] * len(tables) + [vmem] * (1 + len(kvs)),
-        out_specs=vmem,
+        out_specs=[vmem] * len(out_shape),
         compiler_params=VMEM,
-        cost_estimate=pl.CostEstimate(flops=10**9, bytes_accessed=10**6, transcendentals=10**6),
+        cost_estimate=COST,
+        name="attend_first" if first else "attend_second",
     )(*tables, query, *kvs)
 
 
@@ -244,7 +323,7 @@
     smem = pl.BlockSpec(memory_space=pltpu.SMEM)
     vmem = pl.BlockSpec(memory_space=pltpu.VMEM)
     gain = norm_gain[None, :]
-    half = norm(tokens, gain, block, lambda: place()[3])
+    half = norm(tokens, gain, block, lambda: place()[3], None)
     rest = norm(tokens, gain, block, lambda: 1 - place()[3])
 
     n_blocks = block_order.shape[0]
@@ -262,17 +341,11 @@
     docs_other = other_tables[block_order.shape[0] :]
 
     q_cols = w_query.shape[1] // 4
-    keys = lax.dynamic_slice_in_dim(w_key, x * HD, HD, 1)
-    values = lax.dynamic_slice_in_dim(w_value, x * HD, HD, 1)
-    kv_cols = [jnp.where(b == 0, keys, values), jnp.where(b == 0, values, keys)]
-    q_parts = [
-        lax.dynamic_slice_in_dim(w_query, (x * 2 + parity) * q_cols, q_cols, 1)
-        for parity in (b, 1 - b)
-    ]
+    near, kv_same, q_same, kv_other, q_other = cut(w_query, w_key, w_value, q_cols)
+    kv_cols, q_parts = [kv_same, kv_other], [q_same, q_other]
 
     tok_z = swap_seq(half, 2)
     tok_x = swap_group(half)
-    near = jnp.concatenate([kv_cols[0], q_parts[0]], axis=1)
     both_y0 = swap_seq(near, 1)
     kv_z = [near] + [swap_seq(kv_cols[d % 2], 2 * d) for d in range(1, planes)]
     q_z = [near] + [swap_seq(q_parts[d % 2], 2 * d) for d in range(1, planes)]
@@ -296,20 +369,26 @@
     kv_all = [v for part in (kvx_z, kvx_y) for v in part]
 
     last = 2 if planes > 2 else 1
-    (q_acc,) = project(
-        "part", rows, q_acc,
-        q_z[1:] + [q_y[d] for d in range(1, planes) if d != last],
-        [2 * d for d in range(1, planes)] + [2 * d + 1 for d in range(1, planes) if d != last],
-        orders,
-    )
+    firsts = [(q_z[d], 2 * d) for d in range(1, planes) if d != last or planes == 2]
+    thens = [] if planes == 2 else [(q_z[last], 2 * last)]
+    thens += [(q_y[d], 2 * d + 1) for d in range(1, planes) if d != last]
+    left = rows
+    for n, part in enumerate((firsts, thens)):
+        if part:
+            done = project(
+                "part", rows, q_acc, [v for v, _ in part], [m for _, m in part], orders,
+                ahead=2 * last + 1 if n else None,
+            )
+            q_acc = done[0]
+            left = done[1] if n else left
     q_keep, q_give = project(
-        "query", rows, q_acc, [q_y[last]], [2 * last + 1], orders, spin
+        "query", left, q_acc, [q_y[last]], [2 * last + 1], orders, spin
     )
     q_got = swap_seq(q_give, 2)
 
     tables = (block_order, block_docs, order_other, docs_other)
-    att_keep = attend(tables, q_keep, kv_all, kv_masks)
-    att_got = attend(tables, q_got, kv_all, kv_masks)
+    att_keep, key_all, value_all = attend(True, tables, q_keep, kv_all, kv_masks)
+    (att_got,) = attend(False, tables, q_got, (key_all, value_all), kv_masks)
     att = [att_keep, att_got]
     attended = jnp.concatenate(
         [jnp.where(b == 0, att[0], att[1]), jnp.where(b == 0, att[1], att[0])], axis=1

time: 111 us -> 113 us (1.018)
  the two profiles are of different devices: /device:TPU:2 before, /device:TPU:8 now
where the time goes in v1:
time: 113 us
  waiting for transfers between devices  52.8 us (47%)
  starting transfers between devices  33.7 us (30%)
  Pallas kernels  16.1 us (14%)
  local copies, waits for them, and re-layouts  4.29 us (4%)
  other arithmetic  4.29 us (4%)
    ppermute x22, waiting for transfers between devices, swap_seq(): return lax.ppermute(v, 'seq', [(j, j ^ mask) for j in range(n_seq)])  36.9 us
    ppermute x22, starting transfers between devices, swap_seq(): return lax.ppermute(v, 'seq', [(j, j ^ mask) for j in range(n_seq)])  25.2 us
    ppermute x3, waiting for transfers between devices, swap_group(): return lax.ppermute(v, 'groups', [(j, j ^ 1) for j in range(groups)])  12 us
    pallas_call x4, Pallas kernels, project(): pl.pallas_call(functools.partial(project_kernel, masks, mode, ahead), out...  5.64 us
    unnamed x26, local copies, waits for them, and re-layouts  4.21 us
    ppermute x1, waiting for transfers between devices, per_device(): from_b = lax.ppermute(at_other, ('groups', 'seq'), perm_b)  3.93 us
    pallas_call x2, Pallas kernels, attend(): pl.pallas_call(functools.partial(attend_kernel, kv_masks, 1.0 / math.sqrt...  3.61 us
    ppermute x3, starting transfers between devices, swap_group(): return lax.ppermute(v, 'groups', [(j, j ^ 1) for j in range(groups)])  3.52 us
  transfers between devices with their start and end apart: 31, of which 12 were waited for; matrix products, arithmetic and copies ran while one was open for 3% of the time, Pallas kernels for 12%

profile of v1, /device:TPU:8, one launch (start us, length us, event | category | flops | bytes accessed | tf_op | source)
XLA Modules:
  0.0 112.5 jit_solution(11678895145274943735)
XLA Ops:
  0.7 2.2 %norm.2.refs_0_ = bf16[64,4096]{1,0:T(8,128)(2,1)} custom-call(bf16[128,4096]{1,0:T(8,128)(2,1)} %tok.3, f32[1,4096]{1,0:T(1,128)} %bitcast.9), custom_call_target="tpu_custom_call" | custom-call | flops 1024 | bytes 1024 | tf_op jit(solution)/shard_map/norm/pallas_call | solution.py:218
  2.9 2.4 %cut.1 = (bf16[512,384]{1,0:T(8,128)(2,1)}, bf16[512,128]{1,0:T(8,128)(2,1)}, bf16[512,256]{1,0:T(8,128)(2,1)}, bf16[512,128]{1,0:T(8,128)(2,1)}, bf16[512,256]{1,0:T(8,128)(2,1)}) custom-call(bf16[512,1024]{1,0:T(8,128)(2,1)} %w_query.1, bf16[512,256]{1,0:T(8,128)(2,1)} %w_key.1, bf16[512,256]{1,0:T(8,128)(2,1)} %w_value.1), custom_call_target="tpu_custom_call" | custom-call | flops 1024 | bytes 1024 | tf_op jit(solution)/shard_map/cut/pallas_call | solution.py:191
  5.4 3.1 %collective-permute-start.10 = (bf16[512,128]{1,0:T(8,128)(2,1)}, bf16[512,128]{1,0:T(8,128)(2,1)S(1)}, u32[]{:S(2)}, u32[]{:S(2)}) collective-permute-start(bf16[512,128]{1,0:T(8,128)(2,1)} %get-tuple-element.24), channel_id=1, source_target_pairs={{0,12},{2,14},{4,8},{6,10},{8,4},{10,6},{12,0},{14,2},{1,13},{3,15... | collective-permute-start | bytes 393224 | tf_op jit(solution)/shard_map/ppermute | solution.py:315
  11.4 6.5 %collective-permute-done.1.refs_1_ = bf16[64,4096]{1,0:T(8,128)(2,1)S(1)} collective-permute-done((bf16[64,4096]{1,0:T(8,128)(2,1)}, bf16[64,4096]{1,0:T(8,128)(2,1)S(1)}, u32[]{:S(2)}, u32[]{:S(2)}) %collective-permute-start.1) | collective-permute-done | bytes 524320 | tf_op jit(solution)/shard_map/ppermute | solution.py:315
  19.4 1.9 %multiply_cosine_fusion = (f32[16,1,64,64]{3,2,1,0:T(8,128)S(1)}, f32[16,1,64,64]{3,2,1,0:T(8,128)S(1)}, f32[16,1,64,64]{3,2,1,0:T(8,128)S(1)}) fusion(f32[64]{0:T(128)S(1)} %multiply_power_fusion, f32[16,64]{1,0:T(8,128)S(1)} %add_convert_fusion), kind=kLoop, calls=%fused_computation.4 | loop fusion | flops 131072 | bytes 790784 | tf_op jit(solution)/shard_map/cos | solution.py:332
  22.3 12.0 %collective-permute-done = s32[32]{0:T(128)S(1)} collective-permute-done((s32[32]{0:T(128)S(1)}, s32[32]{0:T(128)S(1)}, u32[]{:S(2)}, u32[]{:S(2)}) %collective-permute-start) | collective-permute-done | bytes 160 | tf_op jit(solution)/shard_map/ppermute | solution.py:318
  37.7 3.9 %collective-permute-done.9.refs_11_ = bf16[512,128]{1,0:T(8,128)(2,1)S(1)} collective-permute-done((bf16[512,128]{1,0:T(8,128)(2,1)S(1)}, bf16[512,128]{1,0:T(8,128)(2,1)S(1)}, u32[]{:S(2)}, u32[]{:S(2)}) %collective-permute-start.9) | collective-permute-done | bytes 131104 | tf_op jit(solution)/shard_map/ppermute | solution.py:315
  42.6 3.1 %collective-permute-done.11.refs_0_ = bf16[512,256]{1,0:T(8,128)(2,1)S(1)} collective-permute-done((bf16[512,256]{1,0:T(8,128)(2,1)S(1)}, bf16[512,256]{1,0:T(8,128)(2,1)S(1)}, u32[]{:S(2)}, u32[]{:S(2)}) %collective-permute-start.11) | collective-permute-done | bytes 262176 | tf_op jit(solution)/shard_map/ppermute | solution.py:315
  47.2 9.7 %collective-permute-done.12.refs_1_ = bf16[512,256]{1,0:T(8,128)(2,1)S(1)} collective-permute-done((bf16[512,256]{1,0:T(8,128)(2,1)S(1)}, bf16[512,256]{1,0:T(8,128)(2,1)S(1)}, u32[]{:S(2)}, u32[]{:S(2)}) %collective-permute-start.12) | collective-permute-done | bytes 262176 | tf_op jit(solution)/shard_map/ppermute | solution.py:315
  57.0 7.3 %collective-permute-done.13.refs_0_ = bf16[512,256]{1,0:T(8,128)(2,1)S(1)} collective-permute-done((bf16[512,256]{1,0:T(8,128)(2,1)S(1)}, bf16[512,256]{1,0:T(8,128)(2,1)S(1)}, u32[]{:S(2)}, u32[]{:S(2)}) %collective-permute-start.13) | collective-permute-done | bytes 262176 | tf_op jit(solution)/shard_map/ppermute | solution.py:315
  70.2 1.9 %gather_rows.1 = (bf16[512,4096]{1,0:T(8,128)(2,1)S(1)}, f32[512,128]{1,0:T(8,128)S(1)}, f32[512,256]{1,0:T(8,128)S(1)}, f32[8,2,64,128]{3,2,1,0:T(8,128)S(1)}) custom-call(s32[16]{0:T(128)S(1)} %copy-done.7, s32[16]{0:T(128)S(1)} %get-tuple-element.55.order_other.refs_2_, bf16[64,4096]{1,0:T(8,128)(2,1)S(1)} %copy-done.4, ...), custom_call_target="tpu_custom_call" | custom-call | flops 1024 | bytes 1024 | tf_op jit(solution)/shard_map/gather_rows/pallas_call | solution.py:74
  75.1 1.7 %shard_map.107 = (bf16[4,64,128]{2,1,0:T(8,128)(2,1)S(1)}, bf16[4,64,128]{2,1,0:T(8,128)(2,1)S(1)}) custom-call(s32[16]{0:T(128)S(1)} %copy-done.7, s32[16]{0:T(128)S(1)} %get-tuple-element.55.order_other.refs_2_, bf16[512,4096]{1,0:T(8,128)(2,1)S(1)} %get-tuple-element.27.rows, f32[512,128]{1,0:T(8,128)S(1)} %get-tuple-element.35.acc_ref, ...), custom_call_target="tpu_custom_call" | custom-call | flops 1024 | bytes 1024 | tf_op jit(solution)/shard_map/pallas_call | solution.py:138
  76.8 2.0 %copy-done.1 = bf16[512,4096]{1,0:T(8,128)(2,1)} copy-done((bf16[512,4096]{1,0:T(8,128)(2,1)}, bf16[512,4096]{1,0:T(8,128)(2,1)S(1)}, u32[]{:S(2)}) %copy-start.1) | copy-done | bytes 4194328
  78.7 2.0 %collective-permute-start.20 = (bf16[4,64,128]{2,1,0:T(8,128)(2,1)S(1)}, bf16[4,64,128]{2,1,0:T(8,128)(2,1)S(1)}, u32[]{:S(2)}, u32[]{:S(2)}) collective-permute-start(bf16[4,64,128]{2,1,0:T(8,128)(2,1)S(1)} %get-tuple-element.37), channel_id=1, source_target_pairs={{0,4},{2,6},{4,0},{6,2},{8,12},{10,14},{12,8},{14,10},{1,5},{3,7},... | collective-permute-start | bytes 196616 | tf_op jit(solution)/shard_map/ppermute | solution.py:315
  80.8 1.6 %collective-permute-start.22 = (bf16[4,64,128]{2,1,0:T(8,128)(2,1)S(1)}, bf16[4,64,128]{2,1,0:T(8,128)(2,1)S(1)}, u32[]{:S(2)}, u32[]{:S(2)}) collective-permute-start(bf16[4,64,128]{2,1,0:T(8,128)(2,1)S(1)} %get-tuple-element.37), channel_id=1, source_target_pairs={{0,12},{2,14},{4,8},{6,10},{8,4},{10,6},{12,0},{14,2},{1,13},{3,15... | collective-permute-start | bytes 196616 | tf_op jit(solution)/shard_map/ppermute | solution.py:315
  83.4 2.2 %copy-done.2 = bf16[512,4096]{1,0:T(8,128)(2,1)S(1)} copy-done((bf16[512,4096]{1,0:T(8,128)(2,1)S(1)}, bf16[512,4096]{1,0:T(8,128)(2,1)}, u32[]{:S(2)}) %copy-start.2) | copy-done | bytes 4194328
  86.6 1.6 %collective-permute-start.23 = (bf16[4,64,128]{2,1,0:T(8,128)(2,1)S(1)}, bf16[4,64,128]{2,1,0:T(8,128)(2,1)S(1)}, u32[]{:S(2)}, u32[]{:S(2)}) collective-permute-start(bf16[4,64,128]{2,1,0:T(8,128)(2,1)S(1)} %get-tuple-element.36.refs_5_), channel_id=1, source_target_pairs={{0,2},{2,0},{4,6},{6,4},{8,10},{10,8},{12,14},{14,12},{1,3},{3,1},... | collective-permute-start | bytes 196616 | tf_op jit(solution)/shard_map/ppermute | solution.py:315
  88.2 1.5 %shard_map.105 = (f32[512,256]{1,0:T(8,128)S(1)}, bf16[512,512]{1,0:T(8,128)(2,1)S(1)}) custom-call(s32[16]{0:T(128)S(1)} %copy-done.7, s32[16]{0:T(128)S(1)} %get-tuple-element.55.order_other.refs_2_, bf16[512,4096]{1,0:T(8,128)(2,1)S(1)} %copy-done.2, f32[512,256]{1,0:T(8,128)S(1)} %shard_map.104.acc_ref, ...), custom_call_target="tpu_custom_call" | custom-call | flops 1024 | bytes 1024 | tf_op jit(solution)/shard_map/pallas_call | solution.py:138
  92.9 1.5 %collective-permute-start.25 = (bf16[4,64,128]{2,1,0:T(8,128)(2,1)S(1)}, bf16[4,64,128]{2,1,0:T(8,128)(2,1)S(1)}, u32[]{:S(2)}, u32[]{:S(2)}) collective-permute-start(bf16[4,64,128]{2,1,0:T(8,128)(2,1)S(1)} %collective-permute-done.21.refs_7_), channel_id=1, source_target_pairs={{0,2},{2,0},{4,6},{6,4},{8,10},{10,8},{12,14},{14,12},{1,3},{3,1},... | collective-permute-start | bytes 196616 | tf_op jit(solution)/shard_map/ppermute | solution.py:315
  98.7 1.8 %attend_first.1 = (bf16[256,256]{1,0:T(8,128)(2,1)S(1)}, bf16[16,64,128]{2,1,0:T(8,128)(2,1)S(1)}, bf16[16,64,128]{2,1,0:T(8,128)(2,1)S(1)}) custom-call(s32[16]{0:T(128)S(1)} %copy-done.7, s32[16]{0:T(128)S(1)} %copy-done.8, s32[16]{0:T(128)S(1)} %get-tuple-element.55.order_other.refs_2_, s32[16]{0:T(128)S(1)} %get-tuple-element.54.refs_3_, ...), custom_call_target="tpu_custom_call" | custom-call | flops 1024 | bytes 1024 | tf_op jit(solution)/shard_map/attend_first/pallas_call | solution.py:293
  100.6 1.8 %attend_second.1 = bf16[256,256]{1,0:T(8,128)(2,1)S(1)} custom-call(s32[16]{0:T(128)S(1)} %copy-done.7, s32[16]{0:T(128)S(1)} %copy-done.8, s32[16]{0:T(128)S(1)} %get-tuple-element.55.order_other.refs_2_, s32[16]{0:T(128)S(1)} %get-tuple-element.54.refs_3_, bf16[4,64,256]{2,1,0:T(8,128)(2,1)S(1)} %collective-permute-done.27.refs_4_, ...), custom_call_target="tpu_custom_call" | custom-call | flops 1024 | bytes 1024 | tf_op jit(solution)/shard_map/attend_second/pallas_call | solution.py:293
  102.4 1.6 %collective-permute-start.28 = (bf16[128,512]{1,0:T(8,128)(2,1)S(1)}, bf16[128,512]{1,0:T(8,128)(2,1)S(1)}, u32[]{:S(2)}, u32[]{:S(2)}) collective-permute-start(bf16[128,512]{1,0:T(8,128)(2,1)S(1)} %get-tuple-element.42), channel_id=1, source_target_pairs={{0,4},{2,6},{4,20},{6,22},{8,12},{10,14},{12,28},{14,30},{16,0},{1... | collective-permute-start | bytes 393224 | tf_op jit(solution)/shard_map/ppermute | solution.py:411
  104.0 2.8 %collective-permute-start.29 = (bf16[128,512]{1,0:T(8,128)(2,1)S(1)}, bf16[128,512]{1,0:T(8,128)(2,1)S(1)}, u32[]{:S(2)}, u32[]{:S(2)}) collective-permute-start(bf16[128,512]{1,0:T(8,128)(2,1)S(1)} %get-tuple-element.43), channel_id=1, source_target_pairs={{4,16},{6,18},{12,24},{14,26},{16,4},{18,6},{24,12},{26,14},{5,17}... | collective-permute-start | bytes 393224 | tf_op jit(solution)/shard_map/ppermute | solution.py:412
  107.8 3.9 %collective-permute-done.29 = bf16[128,512]{1,0:T(8,128)(2,1)S(1)} collective-permute-done((bf16[128,512]{1,0:T(8,128)(2,1)S(1)}, bf16[128,512]{1,0:T(8,128)(2,1)S(1)}, u32[]{:S(2)}, u32[]{:S(2)}) %collective-permute-start.29) | collective-permute-done | bytes 131104 | tf_op jit(solution)/shard_map/ppermute | solution.py:412
  (88 shorter events, 31.5 us)
Async XLA Ops:
  2.9 15.0 %collective-permute-start.1 = (bf16[64,4096]{1,0:T(8,128)(2,1)}, bf16[64,4096]{1,0:T(8,128)(2,1)S(1)}, u32[]{:S(2)}, u32[]{:S(2)}) collective-permute-start(bf16[64,4096]{1,0:T(8,128)(2,1)} %norm.2.refs_0_), channel_id=1, source_target_pairs={{0,4},{2,6},{4,0},{6,2},{8,12},{10,14},{12,8},{14,10},{1,5},{3,7},... | collective-permute-start | bytes 1572872 | tf_op jit(solution)/shard_map/ppermute | solution.py:315
  5.4 29.3 %collective-permute-start.10 = (bf16[512,128]{1,0:T(8,128)(2,1)}, bf16[512,128]{1,0:T(8,128)(2,1)S(1)}, u32[]{:S(2)}, u32[]{:S(2)}) collective-permute-start(bf16[512,128]{1,0:T(8,128)(2,1)} %get-tuple-element.24), channel_id=1, source_target_pairs={{0,12},{2,14},{4,8},{6,10},{8,4},{10,6},{12,0},{14,2},{1,13},{3,15... | collective-permute-start | bytes 393224 | tf_op jit(solution)/shard_map/ppermute | solution.py:315
  8.6 27.6 %collective-permute-start.8 = (bf16[512,128]{1,0:T(8,128)(2,1)}, bf16[512,128]{1,0:T(8,128)(2,1)S(1)}, u32[]{:S(2)}, u32[]{:S(2)}) collective-permute-start(bf16[512,128]{1,0:T(8,128)(2,1)} %get-tuple-element.24), channel_id=1, source_target_pairs={{0,4},{2,6},{4,0},{6,2},{8,12},{10,14},{12,8},{14,10},{1,5},{3,7},... | collective-permute-start | bytes 393224 | tf_op jit(solution)/shard_map/ppermute | solution.py:315
  9.9 32.1 %collective-permute-start.2 = (bf16[64,4096]{1,0:T(8,128)(2,1)}, bf16[64,4096]{1,0:T(8,128)(2,1)S(1)}, u32[]{:S(2)}, u32[]{:S(2)}) collective-permute-start(bf16[64,4096]{1,0:T(8,128)(2,1)} %norm.2.refs_0_), channel_id=1, source_target_pairs={{0,16},{16,0},{1,17},{17,1},{2,18},{18,2},{3,19},{19,3},{4,20},{20... | collective-permute-start | bytes 1572872 | tf_op jit(solution)/shard_map/ppermute | solution.py:318
  17.9 24.6 %collective-permute-start.3 = (bf16[64,4096]{1,0:T(8,128)(2,1)S(1)}, bf16[64,4096]{1,0:T(8,128)(2,1)S(1)}, u32[]{:S(2)}, u32[]{:S(2)}) collective-permute-start(bf16[64,4096]{1,0:T(8,128)(2,1)S(1)} %collective-permute-done.1.refs_1_), channel_id=1, source_target_pairs={{0,16},{16,0},{1,17},{17,1},{2,18},{18,2},{3,19},{19,3},{4,20},{20... | collective-permute-start | bytes 1572872 | tf_op jit(solution)/shard_map/ppermute | solution.py:318
  21.8 12.5 %collective-permute-start = (s32[32]{0:T(128)S(1)}, s32[32]{0:T(128)S(1)}, u32[]{:S(2)}, u32[]{:S(2)}) collective-permute-start(s32[32]{0:T(128)S(1)} %pad_add_fusion), channel_id=1, source_target_pairs={{0,16},{16,0},{1,17},{17,1},{2,18},{18,2},{3,19},{19,3},{4,20},{20... | collective-permute-start | bytes 392 | tf_op jit(solution)/shard_map/ppermute | solution.py:318
  34.8 10.9 %collective-permute-start.11 = (bf16[512,256]{1,0:T(8,128)(2,1)S(1)}, bf16[512,256]{1,0:T(8,128)(2,1)S(1)}, u32[]{:S(2)}, u32[]{:S(2)}) collective-permute-start(bf16[512,256]{1,0:T(8,128)(2,1)S(1)} %copy-done.10), channel_id=1, source_target_pairs={{0,4},{2,6},{4,0},{6,2},{8,12},{10,14},{12,8},{14,10},{1,5},{3,7},... | collective-permute-start | bytes 786440 | tf_op jit(solution)/shard_map/ppermute | solution.py:315
  41.6 15.4 %collective-permute-start.12 = (bf16[512,256]{1,0:T(8,128)(2,1)S(1)}, bf16[512,256]{1,0:T(8,128)(2,1)S(1)}, u32[]{:S(2)}, u32[]{:S(2)}) collective-permute-start(bf16[512,256]{1,0:T(8,128)(2,1)S(1)} %copy-done.10), channel_id=1, source_target_pairs={{0,12},{2,14},{4,8},{6,10},{8,4},{10,6},{12,0},{14,2},{1,13},{3,15... | collective-permute-start | bytes 786440 | tf_op jit(solution)/shard_map/ppermute | solution.py:315
  42.0 24.6 %collective-permute-start.4 = (bf16[64,4096]{1,0:T(8,128)(2,1)S(1)}, bf16[64,4096]{1,0:T(8,128)(2,1)S(1)}, u32[]{:S(2)}, u32[]{:S(2)}) collective-permute-start(bf16[64,4096]{1,0:T(8,128)(2,1)S(1)} %collective-permute-done.1.refs_1_), channel_id=1, source_target_pairs={{0,1},{1,0},{2,3},{3,2},{4,5},{5,4},{6,7},{7,6},{8,9},{9,8},{10,11... | collective-permute-start | bytes 1572872 | tf_op jit(solution)/shard_map/ppermute | solution.py:321
  42.0 26.1 %collective-permute-start.5 = (bf16[64,4096]{1,0:T(8,128)(2,1)S(1)}, bf16[64,4096]{1,0:T(8,128)(2,1)S(1)}, u32[]{:S(2)}, u32[]{:S(2)}) collective-permute-start(bf16[64,4096]{1,0:T(8,128)(2,1)S(1)} %collective-permute-done.2.refs_2_), channel_id=1, source_target_pairs={{0,1},{1,0},{2,3},{3,2},{4,5},{5,4},{6,7},{7,6},{8,9},{9,8},{10,11... | collective-permute-start | bytes 1572872 | tf_op jit(solution)/shard_map/ppermute | solution.py:321
  42.6 26.1 %collective-permute-start.6 = (bf16[64,4096]{1,0:T(8,128)(2,1)S(1)}, bf16[64,4096]{1,0:T(8,128)(2,1)S(1)}, u32[]{:S(2)}, u32[]{:S(2)}) collective-permute-start(bf16[64,4096]{1,0:T(8,128)(2,1)S(1)} %collective-permute-done.3.refs_3_), channel_id=1, source_target_pairs={{0,1},{1,0},{2,3},{3,2},{4,5},{5,4},{6,7},{7,6},{8,9},{9,8},{10,11... | collective-permute-start | bytes 1572872 | tf_op jit(solution)/shard_map/ppermute | solution.py:321
  45.7 20.3 %collective-permute-start.7 = (bf16[512,384]{1,0:T(8,128)(2,1)S(1)}, bf16[512,384]{1,0:T(8,128)(2,1)S(1)}, u32[]{:S(2)}, u32[]{:S(2)}) collective-permute-start(bf16[512,384]{1,0:T(8,128)(2,1)S(1)} %copy-done.5), channel_id=1, source_target_pairs={{0,2},{2,0},{4,6},{6,4},{8,10},{10,8},{12,14},{14,12},{1,3},{3,1},... | collective-permute-start | bytes 1179656 | tf_op jit(solution)/shard_map/ppermute | solution.py:315
  64.2 18.2 %collective-permute-start.14 = (bf16[512,256]{1,0:T(8,128)(2,1)S(1)}, bf16[512,256]{1,0:T(8,128)(2,1)S(1)}, u32[]{:S(2)}, u32[]{:S(2)}) collective-permute-start(bf16[512,256]{1,0:T(8,128)(2,1)S(1)} %collective-permute-done.11.refs_0_), channel_id=1, source_target_pairs={{0,2},{2,0},{4,6},{6,4},{8,10},{10,8},{12,14},{14,12},{1,3},{3,1},... | collective-permute-start | bytes 786440 | tf_op jit(solution)/shard_map/ppermute | solution.py:315
  66.0 7.6 %collective-permute-start.19 = (bf16[512,128]{1,0:T(8,128)(2,1)S(1)}, bf16[512,128]{1,0:T(8,128)(2,1)S(1)}, u32[]{:S(2)}, u32[]{:S(2)}) collective-permute-start(bf16[512,128]{1,0:T(8,128)(2,1)S(1)} %collective-permute-done.10.refs_12_), channel_id=1, source_target_pairs={{0,2},{2,0},{4,6},{6,4},{8,10},{10,8},{12,14},{14,12},{1,3},{3,1},... | collective-permute-start | bytes 393224 | tf_op jit(solution)/shard_map/ppermute | solution.py:315
  66.6 8.5 %collective-permute-start.18 = (bf16[512,128]{1,0:T(8,128)(2,1)S(1)}, bf16[512,128]{1,0:T(8,128)(2,1)S(1)}, u32[]{:S(2)}, u32[]{:S(2)}) collective-permute-start(bf16[512,128]{1,0:T(8,128)(2,1)S(1)} %collective-permute-done.9.refs_11_), channel_id=1, source_target_pairs={{0,2},{2,0},{4,6},{6,4},{8,10},{10,8},{12,14},{14,12},{1,3},{3,1},... | collective-permute-start | bytes 393224 | tf_op jit(solution)/shard_map/ppermute | solution.py:315
  68.1 18.5 %collective-permute-start.15 = (bf16[512,256]{1,0:T(8,128)(2,1)S(1)}, bf16[512,256]{1,0:T(8,128)(2,1)}, u32[]{:S(2)}, u32[]{:S(2)}) collective-permute-start(bf16[512,256]{1,0:T(8,128)(2,1)S(1)} %collective-permute-done.12.refs_1_), channel_id=1, source_target_pairs={{0,2},{2,0},{4,6},{6,4},{8,10},{10,8},{12,14},{14,12},{1,3},{3,1},... | collective-permute-start | bytes 786440 | tf_op jit(solution)/shard_map/ppermute | solution.py:315
  68.6 21.1 %collective-permute-start.16 = (bf16[512,256]{1,0:T(8,128)(2,1)S(1)}, bf16[512,256]{1,0:T(8,128)(2,1)S(1)}, u32[]{:S(2)}, u32[]{:S(2)}) collective-permute-start(bf16[512,256]{1,0:T(8,128)(2,1)S(1)} %collective-permute-done.13.refs_0_), channel_id=1, source_target_pairs={{0,2},{2,0},{4,6},{6,4},{8,10},{10,8},{12,14},{14,12},{1,3},{3,1},... | collective-permute-start | bytes 786440 | tf_op jit(solution)/shard_map/ppermute | solution.py:315
  78.7 13.7 %collective-permute-start.20 = (bf16[4,64,128]{2,1,0:T(8,128)(2,1)S(1)}, bf16[4,64,128]{2,1,0:T(8,128)(2,1)S(1)}, u32[]{:S(2)}, u32[]{:S(2)}) collective-permute-start(bf16[4,64,128]{2,1,0:T(8,128)(2,1)S(1)} %get-tuple-element.37), channel_id=1, source_target_pairs={{0,4},{2,6},{4,0},{6,2},{8,12},{10,14},{12,8},{14,10},{1,5},{3,7},... | collective-permute-start | bytes 196616 | tf_op jit(solution)/shard_map/ppermute | solution.py:315
  80.8 13.7 %collective-permute-start.22 = (bf16[4,64,128]{2,1,0:T(8,128)(2,1)S(1)}, bf16[4,64,128]{2,1,0:T(8,128)(2,1)S(1)}, u32[]{:S(2)}, u32[]{:S(2)}) collective-permute-start(bf16[4,64,128]{2,1,0:T(8,128)(2,1)S(1)} %get-tuple-element.37), channel_id=1, source_target_pairs={{0,12},{2,14},{4,8},{6,10},{8,4},{10,6},{12,0},{14,2},{1,13},{3,15... | collective-permute-start | bytes 196616 | tf_op jit(solution)/shard_map/ppermute | solution.py:315
  82.4 10.5 %collective-permute-start.21 = (bf16[4,64,128]{2,1,0:T(8,128)(2,1)S(1)}, bf16[4,64,128]{2,1,0:T(8,128)(2,1)S(1)}, u32[]{:S(2)}, u32[]{:S(2)}) collective-permute-start(bf16[4,64,128]{2,1,0:T(8,128)(2,1)S(1)} %get-tuple-element.36.refs_5_), channel_id=1, source_target_pairs={{0,8},{2,10},{4,12},{6,14},{8,0},{10,2},{12,4},{14,6},{1,9},{3,11}... | collective-permute-start | bytes 196616 | tf_op jit(solution)/shard_map/ppermute | solution.py:315
  86.6 8.5 %collective-permute-start.23 = (bf16[4,64,128]{2,1,0:T(8,128)(2,1)S(1)}, bf16[4,64,128]{2,1,0:T(8,128)(2,1)S(1)}, u32[]{:S(2)}, u32[]{:S(2)}) collective-permute-start(bf16[4,64,128]{2,1,0:T(8,128)(2,1)S(1)} %get-tuple-element.36.refs_5_), channel_id=1, source_target_pairs={{0,2},{2,0},{4,6},{6,4},{8,10},{10,8},{12,14},{14,12},{1,3},{3,1},... | collective-permute-start | bytes 196616 | tf_op jit(solution)/shard_map/ppermute | solution.py:315
  91.2 9.3 %collective-permute-start.27 = (bf16[4,64,256]{2,1,0:T(8,128)(2,1)S(1)}, bf16[4,64,256]{2,1,0:T(8,128)(2,1)S(1)}, u32[]{:S(2)}, u32[]{:S(2)}) collective-permute-start(bf16[4,64,256]{2,1,0:T(8,128)(2,1)S(1)} %get-tuple-element.39), channel_id=1, source_target_pairs={{0,4},{2,6},{4,0},{6,2},{8,12},{10,14},{12,8},{14,10},{1,5},{3,7},... | collective-permute-start | bytes 393224 | tf_op jit(solution)/shard_map/ppermute | solution.py:315
  95.1 11.7 %collective-permute-start.30 = (bf16[64,2,2,128]{3,2,1,0:T(2,128)(2,1)S(1)}, bf16[64,2,2,128]{3,2,1,0:T(2,128)(2,1)S(1)}, u32[]{:S(2)}, u32[]{:S(2)}) collective-permute-start(bf16[64,2,2,128]{3,2,1,0:T(2,128)(2,1)S(1)} %broadcast_select_fusion.2), channel_id=1, source_target_pairs={{0,1},{1,0},{2,3},{3,2},{4,5},{5,4},{6,7},{7,6},{8,9},{9,8},{10,11... | collective-permute-start | bytes 196616 | tf_op jit(solution)/shard_map/ppermute | solution.py:321
  104.0 7.7 %collective-permute-start.29 = (bf16[128,512]{1,0:T(8,128)(2,1)S(1)}, bf16[128,512]{1,0:T(8,128)(2,1)S(1)}, u32[]{:S(2)}, u32[]{:S(2)}) collective-permute-start(bf16[128,512]{1,0:T(8,128)(2,1)S(1)} %get-tuple-element.43), channel_id=1, source_target_pairs={{4,16},{6,18},{12,24},{14,26},{16,4},{18,6},{24,12},{26,14},{5,17}... | collective-permute-start | bytes 393224 | tf_op jit(solution)/shard_map/ppermute | solution.py:412
  (20 other events, 526.1 us)

commit v2 on v1

--- a/solution.py
+++ b/solution.py
@@ -20,15 +20,16 @@
     return g % 2, i, lax.div(i, 2) % 2, c
 
 
-def sources(order_own, order_other):
+def sources(tables=None):
     x, i, b, c = place()
     found = []
     for k in range(8):
         grp = x if k % 4 < 2 else 1 - x
         par = b if k % 4 in (0, 2) else 1 - b
         part = c if k < 4 else 1 - c
-        slot = (i - 2 * b + 2 * par) * 2 + part
-        nat = order_own[slot] if k % 4 < 2 else order_other[slot]
+        nat = None
+        if tables is not None:
+            nat = tables[0 if k % 4 < 2 else 1][(i - 2 * b + 2 * par) * 2 + part]
         found.append((nat, grp == b, par * 2 + part))
     return found
 
@@ -50,7 +51,7 @@
     block = toks[0].shape[0]
     for n, tok in enumerate(toks):
         rows[n * block : (n + 1) * block, :] = tok[...]
-    for k, (nat, _, _) in enumerate(sources(order_own, order_other)):
+    for k, (nat, _, _) in enumerate(sources((order_own, order_other))):
         spin[k] = rope[nat]
     width = both[0].shape[1]
     acc = None
@@ -87,9 +88,10 @@
     )(*orders, *args)
 
 
-def project_kernel(masks, mode, ahead, order_own, order_other, rows, acc_ref, *refs):
+def project_kernel(masks, mode, ahead, *refs):
     _, i, b, _ = place()
-    blks, refs = refs[: len(masks)], refs[len(masks) :]
+    rows, acc_ref = refs[:2]
+    blks, refs = refs[2 : 2 + len(masks)], refs[2 + len(masks) :]
     acc = acc_ref[...]
     depth = blks[0].shape[0]
     for blk, mask in zip(blks, masks):
@@ -103,7 +105,7 @@
         return
     spin, keep, give = refs
     block, heads = keep.shape[1], keep.shape[2] // HD
-    for k, (_, kept, spot) in enumerate(sources(order_own, order_other)):
+    for k, (_, kept, spot) in enumerate(sources()):
         cos, sin = spin[k, 0], spin[k, 1]
         tiles = []
         for h in range(heads):
@@ -123,8 +125,7 @@
             give[spot] = value
 
 
-def project(mode, rows, acc, blks, masks, orders, spin=None, ahead=None):
-    smem = pl.BlockSpec(memory_space=pltpu.SMEM)
+def project(mode, rows, acc, blks, masks, spin=None, ahead=None):
     vmem = pl.BlockSpec(memory_space=pltpu.VMEM)
     width = blks[0].shape[1]
     args = [rows, acc] + list(blks) + ([] if spin is None else [spin])
@@ -138,11 +139,11 @@
     return pl.pallas_call(
         functools.partial(project_kernel, masks, mode, ahead),
         out_shape=out_shape,
-        in_specs=[smem] * 2 + [vmem] * len(args),
+        in_specs=[vmem] * len(args),
         out_specs=[vmem] * len(out_shape),
         compiler_params=VMEM,
         cost_estimate=COST,
-    )(*orders, *args)
+    )(*args)
 
 
 def cut_kernel(w_query, w_key, w_value, near, kv_same, q_same, kv_other, q_other, sems):
@@ -230,21 +231,20 @@
     )(tokens, gain)
 
 
-def attend_kernel(kv_masks, scale, first, *refs):
+def attend_kernel(kv_masks, scale, first, own_tables, other_tables, query_ref, *refs):
     x, i, b, _ = place()
-    order_own, docs_own, order_other, docs_other, query_ref = refs[:5]
     blocks, block, width = query_ref.shape
     heads = width // HD
     base = i - 2 * b
 
-    def table(own, other, index):
-        return jnp.where(x == b, own[index], other[index])
+    def table(index):
+        return jnp.where(x == b, own_tables[index], other_tables[index])
 
     def natural(mask, k):
-        return table(order_own, order_other, ((base ^ mask) + 2 * (k // 2)) * 2 + k % 2)
+        return table(((base ^ mask) + 2 * (k // 2)) * 2 + k % 2)
 
     if first:
-        kvs, (out, key_ref, value_ref) = refs[5:-3], refs[-3:]
+        kvs, (out, key_ref, value_ref) = refs[:-3], refs[-3:]
         for n, mask in enumerate(kv_masks):
             for k in range(blocks):
                 kept, got = kvs[2 * n][k], kvs[2 * n + 1][k]
@@ -252,32 +252,38 @@
                 key_ref[nat] = jnp.where(b == 0, kept, got)
                 value_ref[nat] = jnp.where(b == 0, got, kept)
     else:
-        key_ref, value_ref, out = refs[5:]
+        key_ref, value_ref, out = refs
     total_blocks = key_ref.shape[0]
     window = total_blocks // 2
     lane = lax.broadcasted_iota(jnp.int32, (1, window * block), 1)
     row = lax.broadcasted_iota(jnp.int32, (block, 1), 0)
+    docs = [table(total_blocks + n) for n in range(total_blocks)]
+    tasks = []
     for k in range(blocks):
         nat = natural(0, k)
-        doc = table(docs_own, docs_other, nat)
+        doc = table(total_blocks + nat)
+        opening = jnp.int32(0)
+        for other in docs:
+            opening += (other < doc).astype(jnp.int32)
         start = jnp.maximum(nat - (window - 1), 0)
-        opening = jnp.int32(0)
-        for n in range(total_blocks):
-            opening += (table(docs_own, docs_other, n) < doc).astype(jnp.int32)
         key = key_ref[pl.ds(start, window)].reshape(window * block, HD)
-        value = value_ref[pl.ds(start, window)].reshape(window * block, HD)
         query = jnp.concatenate([query_ref[k, :, h * HD : (h + 1) * HD] for h in range(heads)], axis=0)
         scores = lax.dot_general(
             query, key, (((1,), (1,)), ((), ())), preferred_element_type=jnp.float32
         )
+        tasks.append((nat, opening, start, scores))
+    shares = []
+    for nat, opening, start, scores in tasks:
         key_pos = start * block + lane
         allowed = (key_pos <= nat * block + row) & (key_pos >= opening * block)
         bias = jnp.where(allowed, 0.0, -jnp.inf)
         scores = scores + jnp.concatenate([bias] * heads, axis=0)
         row_max = jnp.max(scores, axis=-1, keepdims=True)
         weights = jnp.exp2((scores - row_max) * (scale * math.log2(math.e)))
-        total = jnp.sum(weights, axis=-1, keepdims=True)
-        mixed = jnp.dot(weights.astype(jnp.bfloat16), value, preferred_element_type=jnp.float32) / total
+        shares.append((weights.astype(jnp.bfloat16), jnp.sum(weights, axis=-1, keepdims=True)))
+    for k, ((_, _, start, _), (weights, total)) in enumerate(zip(tasks, shares)):
+        value = value_ref[pl.ds(start, window)].reshape(window * block, HD)
+        mixed = jnp.dot(weights, value, preferred_element_type=jnp.float32) / total
         out[k * block : (k + 1) * block, :] = jnp.concatenate(
             [mixed[h * block : (h + 1) * block].astype(jnp.bfloat16) for h in range(heads)], axis=1
         )
@@ -289,7 +295,7 @@
     vmem = pl.BlockSpec(memory_space=pltpu.VMEM)
     out_shape = [jax.ShapeDtypeStruct((blocks * block, width), jnp.bfloat16)]
     if first:
-        out_shape += [jax.ShapeDtypeStruct((tables[0].shape[0], block, HD), jnp.bfloat16)] * 2
+        out_shape += [jax.ShapeDtypeStruct((tables[0].shape[0] // 2, block, HD), jnp.bfloat16)] * 2
     return pl.pallas_call(
         functools.partial(attend_kernel, kv_masks, 1.0 / math.sqrt(HD), first),
         out_shape=out_shape,
@@ -337,8 +343,6 @@
     own_tables = jnp.concatenate([block_order, block_docs])
     own_tables, rope = lax.optimization_barrier((own_tables, rope))
     other_tables = swap_group(own_tables)
-    order_other = other_tables[: block_order.shape[0]]
-    docs_other = other_tables[block_order.shape[0] :]
 
     q_cols = w_query.shape[1] // 4
     near, kv_same, q_same, kv_other, q_other = cut(w_query, w_key, w_value, q_cols)
@@ -354,13 +358,13 @@
     tok_xz = swap_group(tok_z)
     toks = [half, tok_z, tok_x, tok_xz, rest] + [swap_core(t) for t in (tok_z, tok_x, tok_xz)]
 
-    orders = (block_order, order_other)
+    orders = (own_tables, other_tables)
 
     rows, kv_acc, q_acc, spin = gather(
         toks, (near, both_y0), (0, 1), kv_z[1:], [2 * d for d in range(1, planes)], orders, rope
     )
     kv_keep, kv_give = project(
-        "key_value", rows, kv_acc, kv_y[1:], [2 * d + 1 for d in range(1, planes)], orders, spin
+        "key_value", rows, kv_acc, kv_y[1:], [2 * d + 1 for d in range(1, planes)], spin
     )
     kvx_z = [kv_keep] + [swap_seq(kv_give if d % 2 else kv_keep, 2 * d) for d in range(1, planes)]
     kvx_y = [swap_seq(kvx_z[d], 1) for d in range(planes)]
@@ -376,17 +380,17 @@
     for n, part in enumerate((firsts, thens)):
         if part:
             done = project(
-                "part", rows, q_acc, [v for v, _ in part], [m for _, m in part], orders,
+                "part", rows, q_acc, [v for v, _ in part], [m for _, m in part],
                 ahead=2 * last + 1 if n else None,
             )
             q_acc = done[0]
             left = done[1] if n else left
     q_keep, q_give = project(
-        "query", left, q_acc, [q_y[last]], [2 * last + 1], orders, spin
+        "query", left, q_acc, [q_y[last]], [2 * last + 1], spin
     )
     q_got = swap_seq(q_give, 2)
 
-    tables = (block_order, block_docs, order_other, docs_other)
+    tables = orders
     att_keep, key_all, value_all = attend(True, tables, q_keep, kv_all, kv_masks)
     (att_got,) = attend(False, tables, q_got, (key_all, value_all), kv_masks)
     att = [att_keep, att_got]

time: 113 us -> 110 us (0.973)
  Pallas kernels: 16.1 us -> 13.3 us
    ppermute x3, waiting for transfers between devices: 12 us -> 13.9 us  [swap_group(): return lax.ppermute(v, 'groups', [(j, j ^ 1) for j in range(groups)])]
    ppermute x22, waiting for transfers between devices: 36.9 us -> 35.1 us  [swap_seq(): return lax.ppermute(v, 'seq', [(j, j ^ mask) for j in range(n_seq)])]
    pallas_call x4, Pallas kernels: 5.64 us -> 4.01 us  [project(): pl.pallas_call(functools.partial(project_kernel, masks, mode, ahead), out...]
    pallas_call x2, Pallas kernels: 3.61 us -> 2.41 us  [attend(): pl.pallas_call(functools.partial(attend_kernel, kv_masks, 1.0 / math.sqrt...]
    unnamed x26 -> x34, local copies, waits for them, and re-layouts: 4.21 us -> 4.23 us
  transfers between devices with their start and end apart: 31 -> 31, of which waited for: 12 -> 12; matrix products, arithmetic and copies ran while one was open for 3% -> 3% of each run, Pallas kernels for 12% -> 10%
where the time goes in v2:
time: 110 us
  waiting for transfers between devices  52.9 us (48%)
  starting transfers between devices  33.7 us (31%)
  Pallas kernels  13.3 us (12%)
  other arithmetic  4.3 us (4%)
  local copies, waits for them, and re-layouts  4.23 us (4%)
    ppermute x22, waiting for transfers between devices, swap_seq(): return lax.ppermute(v, 'seq', [(j, j ^ mask) for j in range(n_seq)])  35.1 us
    ppermute x22, starting transfers between devices, swap_seq(): return lax.ppermute(v, 'seq', [(j, j ^ mask) for j in range(n_seq)])  25.2 us
    ppermute x3, waiting for transfers between devices, swap_group(): return lax.ppermute(v, 'groups', [(j, j ^ 1) for j in range(groups)])  13.9 us
    unnamed x34, local copies, waits for them, and re-layouts  4.23 us
    pallas_call x4, Pallas kernels, project(): pl.pallas_call(functools.partial(project_kernel, masks, mode, ahead), out...  4.01 us
    ppermute x1, waiting for transfers between devices, per_device(): from_b = lax.ppermute(at_other, ('groups', 'seq'), perm_b)  3.94 us
    ppermute x3, starting transfers between devices, swap_group(): return lax.ppermute(v, 'groups', [(j, j ^ 1) for j in range(groups)])  3.53 us
    ppermute x1, starting transfers between devices, per_device(): from_b = lax.ppermute(at_other, ('groups', 'seq'), perm_b)  2.77 us
  transfers between devices with their start and end apart: 31, of which 12 were waited for; matrix products, arithmetic and copies ran while one was open for 3% of the time, Pallas kernels for 10%

profile of v2, /device:TPU:8, one launch (start us, length us, event | category | flops | bytes accessed | tf_op | source)
XLA Modules:
  0.0 109.7 jit_solution(18365305825570603052)
XLA Ops:
  0.7 2.2 %norm.2.refs_0_ = bf16[64,4096]{1,0:T(8,128)(2,1)} custom-call(bf16[128,4096]{1,0:T(8,128)(2,1)} %tok.3, f32[1,4096]{1,0:T(1,128)} %bitcast.9), custom_call_target="tpu_custom_call" | custom-call | flops 1024 | bytes 1024 | tf_op jit(solution)/shard_map/norm/pallas_call | solution.py:219
  2.9 2.4 %cut.1 = (bf16[512,384]{1,0:T(8,128)(2,1)}, bf16[512,128]{1,0:T(8,128)(2,1)}, bf16[512,256]{1,0:T(8,128)(2,1)}, bf16[512,128]{1,0:T(8,128)(2,1)}, bf16[512,256]{1,0:T(8,128)(2,1)}) custom-call(bf16[512,1024]{1,0:T(8,128)(2,1)} %w_query.1, bf16[512,256]{1,0:T(8,128)(2,1)} %w_key.1, bf16[512,256]{1,0:T(8,128)(2,1)} %w_value.1), custom_call_target="tpu_custom_call" | custom-call | flops 1024 | bytes 1024 | tf_op jit(solution)/shard_map/cut/pallas_call | solution.py:192
  5.4 3.1 %collective-permute-start.10 = (bf16[512,128]{1,0:T(8,128)(2,1)}, bf16[512,128]{1,0:T(8,128)(2,1)S(1)}, u32[]{:S(2)}, u32[]{:S(2)}) collective-permute-start(bf16[512,128]{1,0:T(8,128)(2,1)} %get-tuple-element.24), channel_id=1, source_target_pairs={{0,12},{2,14},{4,8},{6,10},{8,4},{10,6},{12,0},{14,2},{1,13},{3,15... | collective-permute-start | bytes 393224 | tf_op jit(solution)/shard_map/ppermute | solution.py:321
  11.4 1.9 %multiply_cosine_fusion = (f32[16,1,64,64]{3,2,1,0:T(8,128)S(1)}, f32[16,1,64,64]{3,2,1,0:T(8,128)S(1)}, f32[16,1,64,64]{3,2,1,0:T(8,128)S(1)}) fusion(f32[64]{0:T(128)S(1)} %multiply_power_fusion, f32[16,64]{1,0:T(8,128)S(1)} %add_convert_fusion), kind=kLoop, calls=%fused_computation.4 | loop fusion | flops 131072 | bytes 790784 | tf_op jit(solution)/shard_map/cos | solution.py:338
  13.3 4.6 %collective-permute-done.1.refs_1_ = bf16[64,4096]{1,0:T(8,128)(2,1)S(1)} collective-permute-done((bf16[64,4096]{1,0:T(8,128)(2,1)}, bf16[64,4096]{1,0:T(8,128)(2,1)S(1)}, u32[]{:S(2)}, u32[]{:S(2)}) %collective-permute-start.1) | collective-permute-done | bytes 524320 | tf_op jit(solution)/shard_map/ppermute | solution.py:321
  20.4 13.9 %collective-permute-done.order_other.other_tables = s32[32]{0:T(128)S(1)} collective-permute-done((s32[32]{0:T(128)S(1)}, s32[32]{0:T(128)S(1)}, u32[]{:S(2)}, u32[]{:S(2)}) %collective-permute-start) | collective-permute-done | bytes 160 | tf_op jit(solution)/shard_map/ppermute | solution.py:324
  36.2 1.5 %collective-permute-start.17 = (bf16[512,128]{1,0:T(8,128)(2,1)S(1)}, bf16[512,128]{1,0:T(8,128)(2,1)S(1)}, u32[]{:S(2)}, u32[]{:S(2)}) collective-permute-start(bf16[512,128]{1,0:T(8,128)(2,1)S(1)} %collective-permute-done.8.refs_10_), channel_id=1, source_target_pairs={{0,2},{2,0},{4,6},{6,4},{8,10},{10,8},{12,14},{14,12},{1,3},{3,1},... | collective-permute-start | bytes 393224 | tf_op jit(solution)/shard_map/ppermute | solution.py:321
  37.7 3.9 %collective-permute-done.9.refs_11_ = bf16[512,128]{1,0:T(8,128)(2,1)S(1)} collective-permute-done((bf16[512,128]{1,0:T(8,128)(2,1)S(1)}, bf16[512,128]{1,0:T(8,128)(2,1)S(1)}, u32[]{:S(2)}, u32[]{:S(2)}) %collective-permute-start.9) | collective-permute-done | bytes 131104 | tf_op jit(solution)/shard_map/ppermute | solution.py:321
  42.6 3.1 %collective-permute-done.11.refs_2_ = bf16[512,256]{1,0:T(8,128)(2,1)S(1)} collective-permute-done((bf16[512,256]{1,0:T(8,128)(2,1)S(1)}, bf16[512,256]{1,0:T(8,128)(2,1)S(1)}, u32[]{:S(2)}, u32[]{:S(2)}) %collective-permute-start.11) | collective-permute-done | bytes 262176 | tf_op jit(solution)/shard_map/ppermute | solution.py:321
  45.7 1.5 %collective-permute-start.7 = (bf16[512,384]{1,0:T(8,128)(2,1)S(1)}, bf16[512,384]{1,0:T(8,128)(2,1)S(1)}, u32[]{:S(2)}, u32[]{:S(2)}) collective-permute-start(bf16[512,384]{1,0:T(8,128)(2,1)S(1)} %copy-done.5), channel_id=1, source_target_pairs={{0,2},{2,0},{4,6},{6,4},{8,10},{10,8},{12,14},{14,12},{1,3},{3,1},... | collective-permute-start | bytes 1179656 | tf_op jit(solution)/shard_map/ppermute | solution.py:321
  47.2 9.7 %collective-permute-done.12.refs_3_ = bf16[512,256]{1,0:T(8,128)(2,1)S(1)} collective-permute-done((bf16[512,256]{1,0:T(8,128)(2,1)S(1)}, bf16[512,256]{1,0:T(8,128)(2,1)S(1)}, u32[]{:S(2)}, u32[]{:S(2)}) %collective-permute-start.12) | collective-permute-done | bytes 262176 | tf_op jit(solution)/shard_map/ppermute | solution.py:321
  56.9 7.3 %collective-permute-done.13.refs_2_ = bf16[512,256]{1,0:T(8,128)(2,1)S(1)} collective-permute-done((bf16[512,256]{1,0:T(8,128)(2,1)S(1)}, bf16[512,256]{1,0:T(8,128)(2,1)S(1)}, u32[]{:S(2)}, u32[]{:S(2)}) %collective-permute-start.13) | collective-permute-done | bytes 262176 | tf_op jit(solution)/shard_map/ppermute | solution.py:321
  70.1 2.0 %gather_rows.1 = (bf16[512,4096]{1,0:T(8,128)(2,1)S(1)}, f32[512,128]{1,0:T(8,128)S(1)}, f32[512,256]{1,0:T(8,128)S(1)}, f32[8,2,64,128]{3,2,1,0:T(8,128)S(1)}) custom-call(s32[32]{0:T(128)S(1)} %pad_add_fusion.order_own.own_tables, s32[32]{0:T(128)S(1)} %collective-permute-done.order_other.other_tables, bf16[64,4096]{1,0:T(8,128)(2,1)S(1)} %copy-done.4, ...), custom_call_target="tpu_custom_call" | custom-call | flops 1024 | bytes 1024 | tf_op jit(solution)/shard_map/gather_rows/pallas_call | solution.py:75
  72.1 1.6 %collective-permute-done.19.refs_4_ = bf16[512,128]{1,0:T(8,128)(2,1)S(1)} collective-permute-done((bf16[512,128]{1,0:T(8,128)(2,1)S(1)}, bf16[512,128]{1,0:T(8,128)(2,1)S(1)}, u32[]{:S(2)}, u32[]{:S(2)}) %collective-permute-start.19) | collective-permute-done | bytes 131104 | tf_op jit(solution)/shard_map/ppermute | solution.py:321
  76.2 2.0 %copy-done.1 = bf16[512,4096]{1,0:T(8,128)(2,1)} copy-done((bf16[512,4096]{1,0:T(8,128)(2,1)}, bf16[512,4096]{1,0:T(8,128)(2,1)S(1)}, u32[]{:S(2)}) %copy-start.1) | copy-done | bytes 4194328
  78.2 2.0 %collective-permute-start.20 = (bf16[4,64,128]{2,1,0:T(8,128)(2,1)S(1)}, bf16[4,64,128]{2,1,0:T(8,128)(2,1)S(1)}, u32[]{:S(2)}, u32[]{:S(2)}) collective-permute-start(bf16[4,64,128]{2,1,0:T(8,128)(2,1)S(1)} %get-tuple-element.37), channel_id=1, source_target_pairs={{0,4},{2,6},{4,0},{6,2},{8,12},{10,14},{12,8},{14,10},{1,5},{3,7},... | collective-permute-start | bytes 196616 | tf_op jit(solution)/shard_map/ppermute | solution.py:321
  80.2 1.6 %collective-permute-start.22 = (bf16[4,64,128]{2,1,0:T(8,128)(2,1)S(1)}, bf16[4,64,128]{2,1,0:T(8,128)(2,1)S(1)}, u32[]{:S(2)}, u32[]{:S(2)}) collective-permute-start(bf16[4,64,128]{2,1,0:T(8,128)(2,1)S(1)} %get-tuple-element.37), channel_id=1, source_target_pairs={{0,12},{2,14},{4,8},{6,10},{8,4},{10,6},{12,0},{14,2},{1,13},{3,15... | collective-permute-start | bytes 196616 | tf_op jit(solution)/shard_map/ppermute | solution.py:321
  82.9 2.2 %copy-done.2 = bf16[512,4096]{1,0:T(8,128)(2,1)S(1)} copy-done((bf16[512,4096]{1,0:T(8,128)(2,1)S(1)}, bf16[512,4096]{1,0:T(8,128)(2,1)}, u32[]{:S(2)}) %copy-start.2) | copy-done | bytes 4194328
  85.6 1.6 %collective-permute-start.23 = (bf16[4,64,128]{2,1,0:T(8,128)(2,1)S(1)}, bf16[4,64,128]{2,1,0:T(8,128)(2,1)S(1)}, u32[]{:S(2)}, u32[]{:S(2)}) collective-permute-start(bf16[4,64,128]{2,1,0:T(8,128)(2,1)S(1)} %get-tuple-element.36.refs_0_), channel_id=1, source_target_pairs={{0,2},{2,0},{4,6},{6,4},{8,10},{10,8},{12,14},{14,12},{1,3},{3,1},... | collective-permute-start | bytes 196616 | tf_op jit(solution)/shard_map/ppermute | solution.py:321
  87.2 1.5 %shard_map.105 = (f32[512,256]{1,0:T(8,128)S(1)}, bf16[512,512]{1,0:T(8,128)(2,1)S(1)}) custom-call(bf16[512,4096]{1,0:T(8,128)(2,1)S(1)} %copy-done.2, f32[512,256]{1,0:T(8,128)S(1)} %shard_map.104.refs_1_, bf16[512,256]{1,0:T(8,128)(2,1)S(1)} %collective-permute-done.13.refs_2_, bf16[512,256]{1,0:T(8,128)(2,1)S(1)} %collective-permute-done.14.refs_3_, ...), custom_call_target="tpu_custom_call" | custom-call | flops 1024 | bytes 1024 | tf_op jit(solution)/shard_map/pallas_call | solution.py:139
  91.3 1.5 %collective-permute-start.25 = (bf16[4,64,128]{2,1,0:T(8,128)(2,1)S(1)}, bf16[4,64,128]{2,1,0:T(8,128)(2,1)S(1)}, u32[]{:S(2)}, u32[]{:S(2)}) collective-permute-start(bf16[4,64,128]{2,1,0:T(8,128)(2,1)S(1)} %collective-permute-done.21.refs_2_), channel_id=1, source_target_pairs={{0,2},{2,0},{4,6},{6,4},{8,10},{10,8},{12,14},{14,12},{1,3},{3,1},... | collective-permute-start | bytes 196616 | tf_op jit(solution)/shard_map/ppermute | solution.py:321
  99.6 1.5 %collective-permute-start.28 = (bf16[128,512]{1,0:T(8,128)(2,1)S(1)}, bf16[128,512]{1,0:T(8,128)(2,1)S(1)}, u32[]{:S(2)}, u32[]{:S(2)}) collective-permute-start(bf16[128,512]{1,0:T(8,128)(2,1)S(1)} %get-tuple-element.42), channel_id=1, source_target_pairs={{0,4},{2,6},{4,20},{6,22},{8,12},{10,14},{12,28},{14,30},{16,0},{1... | collective-permute-start | bytes 393224 | tf_op jit(solution)/shard_map/ppermute | solution.py:415
  101.2 2.8 %collective-permute-start.29 = (bf16[128,512]{1,0:T(8,128)(2,1)S(1)}, bf16[128,512]{1,0:T(8,128)(2,1)S(1)}, u32[]{:S(2)}, u32[]{:S(2)}) collective-permute-start(bf16[128,512]{1,0:T(8,128)(2,1)S(1)} %get-tuple-element.43), channel_id=1, source_target_pairs={{4,16},{6,18},{12,24},{14,26},{16,4},{18,6},{24,12},{26,14},{5,17}... | collective-permute-start | bytes 393224 | tf_op jit(solution)/shard_map/ppermute | solution.py:416
  105.0 3.9 %collective-permute-done.29 = bf16[128,512]{1,0:T(8,128)(2,1)S(1)} collective-permute-done((bf16[128,512]{1,0:T(8,128)(2,1)S(1)}, bf16[128,512]{1,0:T(8,128)(2,1)S(1)}, u32[]{:S(2)}, u32[]{:S(2)}) %collective-permute-start.29) | collective-permute-done | bytes 131104 | tf_op jit(solution)/shard_map/ppermute | solution.py:416
  (95 shorter events, 29.3 us)
Async XLA Ops:
  2.9 15.0 %collective-permute-start.1 = (bf16[64,4096]{1,0:T(8,128)(2,1)}, bf16[64,4096]{1,0:T(8,128)(2,1)S(1)}, u32[]{:S(2)}, u32[]{:S(2)}) collective-permute-start(bf16[64,4096]{1,0:T(8,128)(2,1)} %norm.2.refs_0_), channel_id=1, source_target_pairs={{0,4},{2,6},{4,0},{6,2},{8,12},{10,14},{12,8},{14,10},{1,5},{3,7},... | collective-permute-start | bytes 1572872 | tf_op jit(solution)/shard_map/ppermute | solution.py:321
  5.4 29.3 %collective-permute-start.10 = (bf16[512,128]{1,0:T(8,128)(2,1)}, bf16[512,128]{1,0:T(8,128)(2,1)S(1)}, u32[]{:S(2)}, u32[]{:S(2)}) collective-permute-start(bf16[512,128]{1,0:T(8,128)(2,1)} %get-tuple-element.24), channel_id=1, source_target_pairs={{0,12},{2,14},{4,8},{6,10},{8,4},{10,6},{12,0},{14,2},{1,13},{3,15... | collective-permute-start | bytes 393224 | tf_op jit(solution)/shard_map/ppermute | solution.py:321
  8.5 27.6 %collective-permute-start.8 = (bf16[512,128]{1,0:T(8,128)(2,1)}, bf16[512,128]{1,0:T(8,128)(2,1)S(1)}, u32[]{:S(2)}, u32[]{:S(2)}) collective-permute-start(bf16[512,128]{1,0:T(8,128)(2,1)} %get-tuple-element.24), channel_id=1, source_target_pairs={{0,4},{2,6},{4,0},{6,2},{8,12},{10,14},{12,8},{14,10},{1,5},{3,7},... | collective-permute-start | bytes 393224 | tf_op jit(solution)/shard_map/ppermute | solution.py:321
  9.9 32.1 %collective-permute-start.2 = (bf16[64,4096]{1,0:T(8,128)(2,1)}, bf16[64,4096]{1,0:T(8,128)(2,1)S(1)}, u32[]{:S(2)}, u32[]{:S(2)}) collective-permute-start(bf16[64,4096]{1,0:T(8,128)(2,1)} %norm.2.refs_0_), channel_id=1, source_target_pairs={{0,16},{16,0},{1,17},{17,1},{2,18},{18,2},{3,19},{19,3},{4,20},{20... | collective-permute-start | bytes 1572872 | tf_op jit(solution)/shard_map/ppermute | solution.py:324
  17.9 24.6 %collective-permute-start.3 = (bf16[64,4096]{1,0:T(8,128)(2,1)S(1)}, bf16[64,4096]{1,0:T(8,128)(2,1)S(1)}, u32[]{:S(2)}, u32[]{:S(2)}) collective-permute-start(bf16[64,4096]{1,0:T(8,128)(2,1)S(1)} %collective-permute-done.1.refs_1_), channel_id=1, source_target_pairs={{0,16},{16,0},{1,17},{17,1},{2,18},{18,2},{3,19},{19,3},{4,20},{20... | collective-permute-start | bytes 1572872 | tf_op jit(solution)/shard_map/ppermute | solution.py:324
  19.9 14.4 %collective-permute-start = (s32[32]{0:T(128)S(1)}, s32[32]{0:T(128)S(1)}, u32[]{:S(2)}, u32[]{:S(2)}) collective-permute-start(s32[32]{0:T(128)S(1)} %pad_add_fusion.order_own.own_tables), channel_id=1, source_target_pairs={{0,16},{16,0},{1,17},{17,1},{2,18},{18,2},{3,19},{19,3},{4,20},{20... | collective-permute-start | bytes 392 | tf_op jit(solution)/shard_map/ppermute | solution.py:324
  34.7 10.9 %collective-permute-start.11 = (bf16[512,256]{1,0:T(8,128)(2,1)S(1)}, bf16[512,256]{1,0:T(8,128)(2,1)S(1)}, u32[]{:S(2)}, u32[]{:S(2)}) collective-permute-start(bf16[512,256]{1,0:T(8,128)(2,1)S(1)} %copy-done.12), channel_id=1, source_target_pairs={{0,4},{2,6},{4,0},{6,2},{8,12},{10,14},{12,8},{14,10},{1,5},{3,7},... | collective-permute-start | bytes 786440 | tf_op jit(solution)/shard_map/ppermute | solution.py:321
  41.6 15.4 %collective-permute-start.12 = (bf16[512,256]{1,0:T(8,128)(2,1)S(1)}, bf16[512,256]{1,0:T(8,128)(2,1)S(1)}, u32[]{:S(2)}, u32[]{:S(2)}) collective-permute-start(bf16[512,256]{1,0:T(8,128)(2,1)S(1)} %copy-done.12), channel_id=1, source_target_pairs={{0,12},{2,14},{4,8},{6,10},{8,4},{10,6},{12,0},{14,2},{1,13},{3,15... | collective-permute-start | bytes 786440 | tf_op jit(solution)/shard_map/ppermute | solution.py:321
  42.0 24.2 %collective-permute-start.4 = (bf16[64,4096]{1,0:T(8,128)(2,1)S(1)}, bf16[64,4096]{1,0:T(8,128)(2,1)S(1)}, u32[]{:S(2)}, u32[]{:S(2)}) collective-permute-start(bf16[64,4096]{1,0:T(8,128)(2,1)S(1)} %collective-permute-done.1.refs_1_), channel_id=1, source_target_pairs={{0,1},{1,0},{2,3},{3,2},{4,5},{5,4},{6,7},{7,6},{8,9},{9,8},{10,11... | collective-permute-start | bytes 1572872 | tf_op jit(solution)/shard_map/ppermute | solution.py:327
  42.0 25.7 %collective-permute-start.5 = (bf16[64,4096]{1,0:T(8,128)(2,1)S(1)}, bf16[64,4096]{1,0:T(8,128)(2,1)S(1)}, u32[]{:S(2)}, u32[]{:S(2)}) collective-permute-start(bf16[64,4096]{1,0:T(8,128)(2,1)S(1)} %collective-permute-done.2.refs_2_), channel_id=1, source_target_pairs={{0,1},{1,0},{2,3},{3,2},{4,5},{5,4},{6,7},{7,6},{8,9},{9,8},{10,11... | collective-permute-start | bytes 1572872 | tf_op jit(solution)/shard_map/ppermute | solution.py:327
  42.5 25.7 %collective-permute-start.6 = (bf16[64,4096]{1,0:T(8,128)(2,1)S(1)}, bf16[64,4096]{1,0:T(8,128)(2,1)S(1)}, u32[]{:S(2)}, u32[]{:S(2)}) collective-permute-start(bf16[64,4096]{1,0:T(8,128)(2,1)S(1)} %collective-permute-done.3.refs_3_), channel_id=1, source_target_pairs={{0,1},{1,0},{2,3},{3,2},{4,5},{5,4},{6,7},{7,6},{8,9},{9,8},{10,11... | collective-permute-start | bytes 1572872 | tf_op jit(solution)/shard_map/ppermute | solution.py:327
  45.7 20.1 %collective-permute-start.7 = (bf16[512,384]{1,0:T(8,128)(2,1)S(1)}, bf16[512,384]{1,0:T(8,128)(2,1)S(1)}, u32[]{:S(2)}, u32[]{:S(2)}) collective-permute-start(bf16[512,384]{1,0:T(8,128)(2,1)S(1)} %copy-done.5), channel_id=1, source_target_pairs={{0,2},{2,0},{4,6},{6,4},{8,10},{10,8},{12,14},{14,12},{1,3},{3,1},... | collective-permute-start | bytes 1179656 | tf_op jit(solution)/shard_map/ppermute | solution.py:321
  64.2 17.6 %collective-permute-start.14 = (bf16[512,256]{1,0:T(8,128)(2,1)S(1)}, bf16[512,256]{1,0:T(8,128)(2,1)S(1)}, u32[]{:S(2)}, u32[]{:S(2)}) collective-permute-start(bf16[512,256]{1,0:T(8,128)(2,1)S(1)} %collective-permute-done.11.refs_2_), channel_id=1, source_target_pairs={{0,2},{2,0},{4,6},{6,4},{8,10},{10,8},{12,14},{14,12},{1,3},{3,1},... | collective-permute-start | bytes 786440 | tf_op jit(solution)/shard_map/ppermute | solution.py:321
  65.7 7.9 %collective-permute-start.19 = (bf16[512,128]{1,0:T(8,128)(2,1)S(1)}, bf16[512,128]{1,0:T(8,128)(2,1)S(1)}, u32[]{:S(2)}, u32[]{:S(2)}) collective-permute-start(bf16[512,128]{1,0:T(8,128)(2,1)S(1)} %collective-permute-done.10.refs_12_), channel_id=1, source_target_pairs={{0,2},{2,0},{4,6},{6,4},{8,10},{10,8},{12,14},{14,12},{1,3},{3,1},... | collective-permute-start | bytes 393224 | tf_op jit(solution)/shard_map/ppermute | solution.py:321
  66.2 8.8 %collective-permute-start.18 = (bf16[512,128]{1,0:T(8,128)(2,1)S(1)}, bf16[512,128]{1,0:T(8,128)(2,1)S(1)}, u32[]{:S(2)}, u32[]{:S(2)}) collective-permute-start(bf16[512,128]{1,0:T(8,128)(2,1)S(1)} %collective-permute-done.9.refs_11_), channel_id=1, source_target_pairs={{0,2},{2,0},{4,6},{6,4},{8,10},{10,8},{12,14},{14,12},{1,3},{3,1},... | collective-permute-start | bytes 393224 | tf_op jit(solution)/shard_map/ppermute | solution.py:321
  67.8 17.8 %collective-permute-start.15 = (bf16[512,256]{1,0:T(8,128)(2,1)S(1)}, bf16[512,256]{1,0:T(8,128)(2,1)}, u32[]{:S(2)}, u32[]{:S(2)}) collective-permute-start(bf16[512,256]{1,0:T(8,128)(2,1)S(1)} %collective-permute-done.12.refs_3_), channel_id=1, source_target_pairs={{0,2},{2,0},{4,6},{6,4},{8,10},{10,8},{12,14},{14,12},{1,3},{3,1},... | collective-permute-start | bytes 786440 | tf_op jit(solution)/shard_map/ppermute | solution.py:321
  68.3 20.4 %collective-permute-start.16 = (bf16[512,256]{1,0:T(8,128)(2,1)S(1)}, bf16[512,256]{1,0:T(8,128)(2,1)S(1)}, u32[]{:S(2)}, u32[]{:S(2)}) collective-permute-start(bf16[512,256]{1,0:T(8,128)(2,1)S(1)} %collective-permute-done.13.refs_2_), channel_id=1, source_target_pairs={{0,2},{2,0},{4,6},{6,4},{8,10},{10,8},{12,14},{14,12},{1,3},{3,1},... | collective-permute-start | bytes 786440 | tf_op jit(solution)/shard_map/ppermute | solution.py:321
  78.2 12.6 %collective-permute-start.20 = (bf16[4,64,128]{2,1,0:T(8,128)(2,1)S(1)}, bf16[4,64,128]{2,1,0:T(8,128)(2,1)S(1)}, u32[]{:S(2)}, u32[]{:S(2)}) collective-permute-start(bf16[4,64,128]{2,1,0:T(8,128)(2,1)S(1)} %get-tuple-element.37), channel_id=1, source_target_pairs={{0,4},{2,6},{4,0},{6,2},{8,12},{10,14},{12,8},{14,10},{1,5},{3,7},... | collective-permute-start | bytes 196616 | tf_op jit(solution)/shard_map/ppermute | solution.py:321
  80.2 12.6 %collective-permute-start.22 = (bf16[4,64,128]{2,1,0:T(8,128)(2,1)S(1)}, bf16[4,64,128]{2,1,0:T(8,128)(2,1)S(1)}, u32[]{:S(2)}, u32[]{:S(2)}) collective-permute-start(bf16[4,64,128]{2,1,0:T(8,128)(2,1)S(1)} %get-tuple-element.37), channel_id=1, source_target_pairs={{0,12},{2,14},{4,8},{6,10},{8,4},{10,6},{12,0},{14,2},{1,13},{3,15... | collective-permute-start | bytes 196616 | tf_op jit(solution)/shard_map/ppermute | solution.py:321
  81.9 9.4 %collective-permute-start.21 = (bf16[4,64,128]{2,1,0:T(8,128)(2,1)S(1)}, bf16[4,64,128]{2,1,0:T(8,128)(2,1)S(1)}, u32[]{:S(2)}, u32[]{:S(2)}) collective-permute-start(bf16[4,64,128]{2,1,0:T(8,128)(2,1)S(1)} %get-tuple-element.36.refs_0_), channel_id=1, source_target_pairs={{0,8},{2,10},{4,12},{6,14},{8,0},{10,2},{12,4},{14,6},{1,9},{3,11}... | collective-permute-start | bytes 196616 | tf_op jit(solution)/shard_map/ppermute | solution.py:321
  85.6 7.9 %collective-permute-start.23 = (bf16[4,64,128]{2,1,0:T(8,128)(2,1)S(1)}, bf16[4,64,128]{2,1,0:T(8,128)(2,1)S(1)}, u32[]{:S(2)}, u32[]{:S(2)}) collective-permute-start(bf16[4,64,128]{2,1,0:T(8,128)(2,1)S(1)} %get-tuple-element.36.refs_0_), channel_id=1, source_target_pairs={{0,2},{2,0},{4,6},{6,4},{8,10},{10,8},{12,14},{14,12},{1,3},{3,1},... | collective-permute-start | bytes 196616 | tf_op jit(solution)/shard_map/ppermute | solution.py:321
  89.6 8.8 %collective-permute-start.27 = (bf16[4,64,256]{2,1,0:T(8,128)(2,1)S(1)}, bf16[4,64,256]{2,1,0:T(8,128)(2,1)S(1)}, u32[]{:S(2)}, u32[]{:S(2)}) collective-permute-start(bf16[4,64,256]{2,1,0:T(8,128)(2,1)S(1)} %get-tuple-element.39), channel_id=1, source_target_pairs={{0,4},{2,6},{4,0},{6,2},{8,12},{10,14},{12,8},{14,10},{1,5},{3,7},... | collective-permute-start | bytes 393224 | tf_op jit(solution)/shard_map/ppermute | solution.py:321
  93.5 10.5 %collective-permute-start.30 = (bf16[64,2,2,128]{3,2,1,0:T(2,128)(2,1)S(1)}, bf16[64,2,2,128]{3,2,1,0:T(2,128)(2,1)S(1)}, u32[]{:S(2)}, u32[]{:S(2)}) collective-permute-start(bf16[64,2,2,128]{3,2,1,0:T(2,128)(2,1)S(1)} %broadcast_select_fusion.2), channel_id=1, source_target_pairs={{0,1},{1,0},{2,3},{3,2},{4,5},{5,4},{6,7},{7,6},{8,9},{9,8},{10,11... | collective-permute-start | bytes 196616 | tf_op jit(solution)/shard_map/ppermute | solution.py:327
  101.2 7.7 %collective-permute-start.29 = (bf16[128,512]{1,0:T(8,128)(2,1)S(1)}, bf16[128,512]{1,0:T(8,128)(2,1)S(1)}, u32[]{:S(2)}, u32[]{:S(2)}) collective-permute-start(bf16[128,512]{1,0:T(8,128)(2,1)S(1)} %get-tuple-element.43), channel_id=1, source_target_pairs={{4,16},{6,18},{12,24},{14,26},{16,4},{18,6},{24,12},{26,14},{5,17}... | collective-permute-start | bytes 393224 | tf_op jit(solution)/shard_map/ppermute | solution.py:416
  (24 other events, 650.8 us)
